TPU v7x, 128 devices: a whole 4x4x4 slice. The times are simulated.
128 devices in a mesh: seq: 8 (over x_lo, z), exp: 16 (over x_hi, y, core).
Axes of the slice: x: 4 (x_hi: 2, x_lo: 2; x = x_hi * 2 + x_lo), y: 4, z: 4, core: 2. Of those that a mesh axis runs over, the one named last changes fastest.
Arguments:
- tokens: bfloat16 [16, 1024, 2048], P('exp', 'seq'), may hold values from -6 to 6
- position_of_row: int32 [16, 1024], P('exp'), may hold values from 0 to 1023, each once within a row
- request_of_position: int32 [16, 1024], P('exp'), may hold values from 0 to 3, never falling along the last dimension, each value on 1 to 512 neighbouring positions
- expert_ids: int32 [16, 1024, 6], P('exp', 'seq'), may hold values from 0 to 63, all different within a row; in each aligned block of 128 rows (0 to 127, 128 to 255, ..., all dimensions but the last counted through in order) at most 16 rows name the same one
- gate_values: float32 [16, 1024, 6], P('exp', 'seq'), may hold values from 0.1 to 1
- attn_norm: bfloat16 [2048], replicated, may hold values from 0.25 to 1.75
- moe_norm: bfloat16 [2048], replicated, may hold values from 0.25 to 1.75
- w_query: bfloat16 [2048, 2048], P(None, 'seq'), may hold values from -0.125 to 0.125
- w_latent: bfloat16 [2048, 512], replicated, may hold values from -0.125 to 0.125
- w_key_up: bfloat16 [512, 2048], P(None, 'seq'), may hold values from -120 to 120
- w_value_up: bfloat16 [512, 2048], P(None, 'seq'), may hold values from -0.25 to 0.25
- w_output: bfloat16 [2048, 2048], P('seq'), may hold values from -0.125 to 0.125
- w_shared_gate: bfloat16 [2048, 2816], P(None, 'seq'), may hold values from -0.125 to 0.125
- w_shared_up: bfloat16 [2048, 2816], P(None, 'seq'), may hold values from -0.125 to 0.125
- w_shared_down: bfloat16 [2816, 2048], P('seq'), may hold values from -0.109375 to 0.109375
- w_routed_gate: bfloat16 [128, 2048, 704], P(('seq', 'exp')), may hold values from -0.125 to 0.125
- w_routed_up: bfloat16 [128, 2048, 704], P(('seq', 'exp')), may hold values from -0.125 to 0.125
- w_routed_down: bfloat16 [128, 704, 2048], P(('seq', 'exp')), may hold values from -0.15625 to 0.15625
Outputs:
- layer_out: bfloat16 [16, 1024, 2048], P('exp', 'seq')
Inputs may be any that keep to these rules, and one draw needn't show every extreme that they name: `expert_ids`: each row names 6 different experts; among the rows of one device no expert is named by more than 16 rows, and some expert reaches 16 on some device. `position_of_row`: each row of a group holds a different position. `request_of_position`: never falls along positions; each request holds 1 to 512 positions.
All inputs are finite; a program needn't handle non-finite values.
Results may differ from a plain program's by a relative error of at most 0.027.
The roundings to bfloat16 on the way count: a program that leaves them out, or rounds other values in their place, can miss the bound.
Values may be sent and summed in bfloat16 or wider, within the bound.
No kernel may reach another device: no remote copies, remote signals or barrier semaphores. Data moves between devices by JAX's collectives and lax.ppermute only.
A program may use at most 128 MiB of HBM per device.

v0:
```python
import jax
import jax.numpy as jnp
from jax import lax
from jax.experimental import pallas as pl
from jax.experimental.pallas import tpu as pltpu
from jax.sharding import Mesh
from jax.sharding import PartitionSpec as P

HD = 128
LAT = 512
CAP = 16

SEQ = ("xl", "z")
EXP = ("xh", "y", "c")
ALL = SEQ + EXP

epsilon = 1e-06
exponent_scale = 192.0 ** (-0.5) * 1.4426950408889634
f32 = jnp.float32
bf16 = jnp.bfloat16


def ring(count, step):
    return [(i, (i + step) % count) for i in range(count)]


def gather_pieces(own, early=None):
    half = own.shape[0] // 2
    up = ring(4, 1)
    down = ring(4, -1)
    flip = ring(2, 1)
    below = lax.ppermute(own, "z", up)
    above = lax.ppermute(own, "z", down)
    side = lax.ppermute(own, "xl", flip)
    if early is not None:
        side, early = lax.optimization_barrier((side, early))
    far = lax.ppermute(below, "z", up)
    side_below = lax.ppermute(below, "xl", flip)
    side_above = lax.ppermute(side, "z", down)
    side_far_low = lax.ppermute(side_below[:half], "z", up)
    side_far_high = lax.ppermute(side_above[half:], "z", down)
    pieces = (
        (0, 0, 0, own),
        (0, 3, 0, below),
        (0, 1, 0, above),
        (1, 0, 0, side),
        (1, 3, 0, side_below),
        (1, 1, 0, side_above),
        (0, 2, 0, far),
        (1, 2, 0, side_far_low),
        (1, 2, half, side_far_high),
    )
    return pieces, early


def place_of(dx, dz):
    xl = lax.axis_index("xl")
    z = lax.axis_index("z")
    return ((xl + dx) % 2) * 4 + (z + dz) % 4


def gather_rows(own, early):
    rows, width = own.shape
    out = set_down(own, place_of(0, 0), 0)
    pieces, early = gather_pieces(own, early)
    for dx, dz, start, piece in pieces[1:]:
        out = lax.dynamic_update_slice(out, piece, (place_of(dx, dz) * rows + start, 0))
    return out, early


def set_down(own, place, axis):
    def body(place_ref, own_ref, out_ref):
        out_ref[...] = own_ref[...]

    shape = list(own.shape)
    shape[axis] *= 8
    index = (lambda i, p: (p[0], 0)) if axis == 0 else (lambda i, p: (0, p[0]))
    return pl.pallas_call(
        body,
        grid_spec=pltpu.PrefetchScalarGridSpec(
            num_scalar_prefetch=1,
            grid=(1,),
            in_specs=[pl.BlockSpec(own.shape, lambda i, p: (0, 0))],
            out_specs=pl.BlockSpec(own.shape, index),
        ),
        out_shape=jax.ShapeDtypeStruct(shape, own.dtype),
        name="set_down",
    )(place.reshape(1), own)


def gather_columns(own):
    rows, width = own.shape
    out = set_down(own, place_of(0, 0), 1)
    for dx, dz, start, piece in gather_pieces(own)[0][1:]:
        out = lax.dynamic_update_slice(out, piece, (start, place_of(dx, dz) * width))
    return out


def swap_cores(values):
    return lax.ppermute(values, "c", [(0, 1), (1, 0)])


def attention(tokens_all, gain, w_latent, w_query, w_key_up, w_value_up, positions, request_table, block=512):
    rows, width = tokens_all.shape
    heads = w_query.shape[1] // HD
    blocks = rows // block

    def body(
        x_ref,
        gain_ref,
        wl_ref,
        wq_ref,
        wk_ref,
        wv_ref,
        pos_ref,
        table_ref,
        out_ref,
        lat_ref,
        ql_ref,
        marks_ref,
    ):
        phase = pl.program_id(0)
        start = pl.multiple_of(pl.program_id(1) * block, block)

        @pl.when((phase == 0) & (start == 0))
        def _():
            position = pos_ref[...].astype(f32)
            table = table_ref[...].astype(f32)
            request = jnp.zeros_like(position)
            for value in range(1, 4):
                first = jnp.sum((table < value).astype(f32), axis=1, keepdims=True)
                request = request + (position >= first).astype(f32)
            marks_ref[0:1, :] = position
            marks_ref[1:2, :] = request
            marks_ref[2:8, :] = jnp.zeros((6, rows), f32)

        @pl.when(phase == 0)
        def _():
            x = x_ref[...].astype(f32)
            mean_square = jnp.mean(x * x, axis=-1, keepdims=True)
            normed = (x * lax.rsqrt(mean_square + epsilon) * gain_ref[...].astype(f32)).astype(bf16)
            lat = jnp.dot(normed, wl_ref[...], preferred_element_type=f32)
            lat_ref[pl.ds(start, block), :] = lat.astype(bf16)
            queries = jnp.dot(normed, wq_ref[...], preferred_element_type=f32).astype(bf16)
            for head in range(heads):
                cols = slice(head * HD, (head + 1) * HD)
                ql = lax.dot_general(
                    queries[:, cols], wk_ref[:, cols], (((1,), (1,)), ((), ())), preferred_element_type=f32
                )
                ql_ref[head, pl.ds(start, block), :] = ql.astype(bf16)

        @pl.when(phase == 1)
        def _():
            lat = lat_ref[...]
            down = marks_ref[:, pl.ds(start, block)].T
            seen = (marks_ref[0:1, :] <= down[:, 0:1]) & (marks_ref[1:2, :] == down[:, 1:2])
            for head in range(heads):
                cols = slice(head * HD, (head + 1) * HD)
                ql = ql_ref[head, pl.ds(start, block), :]
                scores = lax.dot_general(
                    ql, lat, (((1,), (1,)), ((), ())), preferred_element_type=f32
                )
                scores = jnp.where(seen, scores, -1e30)
                largest = jnp.max(scores, axis=1, keepdims=True)
                raised = jnp.exp2((scores - largest) * exponent_scale)
                total = jnp.sum(raised, axis=1, keepdims=True)
                mixed = jnp.dot(raised.astype(bf16), lat, preferred_element_type=f32)
                mixed = (mixed * (1.0 / total)).astype(bf16)
                head_out = jnp.dot(mixed, wv_ref[:, cols], preferred_element_type=f32).astype(bf16)
                out_ref[:, cols] = head_out

    whole = lambda a: pl.BlockSpec(a.shape, lambda p, i: (0,) * a.ndim)
    late = lambda p, i: jnp.where(p == 0, 0, i)
    return pl.pallas_call(
        body,
        grid_spec=pl.GridSpec(
            grid=(2, blocks),
            in_specs=[
                pl.BlockSpec((block, width), lambda p, i: (jnp.where(p == 0, i, blocks - 1), 0)),
                whole(gain),
                whole(w_latent),
                whole(w_query),
                whole(w_key_up),
                whole(w_value_up),
                whole(positions),
                whole(request_table),
            ],
            out_specs=pl.BlockSpec((block, heads * HD), lambda p, i: (late(p, i), 0)),
            scratch_shapes=[
                pltpu.VMEM((rows, LAT), bf16),
                pltpu.VMEM((heads, rows, LAT), bf16),
                pltpu.VMEM((8, rows), f32),
            ],
        ),
        out_shape=jax.ShapeDtypeStruct((rows, heads * HD), bf16),
        compiler_params=pltpu.CompilerParams(
            dimension_semantics=("arbitrary", "arbitrary"), vmem_limit_bytes=62 * 1024 * 1024
        ),
        name="attend",
    )(
        tokens_all,
        gain,
        w_latent,
        w_query,
        w_key_up,
        w_value_up,
        positions,
        request_table,
    )


def run_dispatch(here, joined, own, w_out, gain, spread, together_of=4, slot_block=512):
    rows, width = own.shape
    pieces, inner, span = w_out.shape
    slots = spread.shape[0]
    first = pieces // together_of
    last = slots // slot_block

    def body(here_ref, j_ref, x_ref, wo_ref, gain_ref, spread_ref, resid_ref, out_ref, moe_ref):
        step = pl.program_id(0)

        @pl.when(step < first)
        def _():
            for part in range(together_of):
                start = (step * together_of + part) * span
                cols = pl.ds(pl.multiple_of(start, span), span)
                attended = jnp.dot(j_ref[...], wo_ref[part], preferred_element_type=f32)
                added = x_ref[:, cols].astype(f32) + attended
                resid_ref[:, cols] = added.astype(bf16)

        @pl.when(step == first)
        def _():
            resid = resid_ref[...].astype(f32)
            mean_square = jnp.mean(resid * resid, axis=-1, keepdims=True)
            normed = resid * lax.rsqrt(mean_square + epsilon) * gain_ref[...].astype(f32)
            moe_ref[...] = normed.astype(bf16)

        @pl.when(step >= first)
        def _():
            out_ref[...] = jnp.dot(
                spread_ref[...], moe_ref[...], preferred_element_type=f32
            ).astype(bf16)

    late = lambda i: jnp.maximum(i - first, 0)
    return pl.pallas_call(
        body,
        grid_spec=pltpu.PrefetchScalarGridSpec(
            num_scalar_prefetch=1,
            grid=(first + last,),
            in_specs=[
                pl.BlockSpec((rows, inner), lambda i, h: (h[0], 0)),
                pl.BlockSpec((rows, width), lambda i, h: (0, 0)),
                pl.BlockSpec(
                    (together_of, inner, span), lambda i, h: (jnp.minimum(i, first - 1), 0, 0)
                ),
                pl.BlockSpec((1, width), lambda i, h: (0, 0)),
                pl.BlockSpec((slot_block, rows), lambda i, h: (late(i), 0)),
            ],
            out_specs=[
                pl.BlockSpec((rows, width), lambda i, h: (0, 0)),
                pl.BlockSpec((slot_block, width), lambda i, h: (late(i), 0)),
            ],
            scratch_shapes=[pltpu.VMEM((rows, width), bf16)],
        ),
        out_shape=[
            jax.ShapeDtypeStruct((rows, width), bf16),
            jax.ShapeDtypeStruct((slots, width), bf16),
        ],
        compiler_params=pltpu.CompilerParams(
            dimension_semantics=("arbitrary",), vmem_limit_bytes=58 * 1024 * 1024
        ),
        name="dispatch",
    )(here.reshape(1), joined, own, w_out, gain, spread)


def run_combine(mixing, returned, resid, shared_out, block=512):
    rows, width = resid.shape

    def body(m_ref, r_ref, resid_ref, shared_ref, out_ref):
        parts = jnp.dot(m_ref[...], r_ref[...], preferred_element_type=f32)
        routed = parts[:rows] + parts[rows : 2 * rows] + parts[2 * rows :]
        total = resid_ref[...].astype(f32) + shared_ref[...].astype(f32) + routed
        out_ref[...] = total.astype(bf16)

    by_cols = lambda a: pl.BlockSpec((a.shape[0], block), lambda i: (0, i))
    return pl.pallas_call(
        body,
        grid=(width // block,),
        in_specs=[
            pl.BlockSpec(mixing.shape, lambda i: (0, 0)),
            by_cols(returned),
            by_cols(resid),
            by_cols(shared_out),
        ],
        out_specs=by_cols(resid),
        out_shape=jax.ShapeDtypeStruct((rows, width), bf16),
        compiler_params=pltpu.CompilerParams(
            dimension_semantics=("arbitrary",), vmem_limit_bytes=58 * 1024 * 1024
        ),
        name="combine",
    )(mixing, returned, resid, shared_out)


def run_shared(joined, tokens_all, w_out, gain, w_gate, w_up, w_down, block=256):
    rows, width = tokens_all.shape
    pieces, _, span = w_out.shape

    def body(j_ref, x_ref, wo_ref, gain_ref, wg_ref, wu_ref, wd_ref, out_ref, res_ref):
        for piece in range(pieces):
            cols = slice(piece * span, (piece + 1) * span)
            attended = jnp.dot(j_ref[...], wo_ref[piece], preferred_element_type=f32)
            added = x_ref[:, cols].astype(f32) + attended
            res_ref[:, cols] = added.astype(bf16)
        resid = res_ref[...].astype(f32)
        mean_square = jnp.mean(resid * resid, axis=-1, keepdims=True)
        moe_in = (resid * lax.rsqrt(mean_square + epsilon) * gain_ref[...].astype(f32)).astype(bf16)
        across = (((1,), (1,)), ((), ()))
        gate = lax.dot_general(moe_in, wg_ref[...], across, preferred_element_type=f32)
        up = lax.dot_general(moe_in, wu_ref[...], across, preferred_element_type=f32)
        act = (gate * (1.0 / (1.0 + jnp.exp(-gate))) * up).astype(bf16)
        out_ref[...] = jnp.dot(act, wd_ref[...], preferred_element_type=f32).astype(bf16)

    whole = lambda a: pl.BlockSpec(a.shape, lambda i: (0,) * a.ndim)
    by_rows = lambda a: pl.BlockSpec((block, a.shape[1]), lambda i: (i, 0))
    operands = (joined, tokens_all, w_out, gain, w_gate, w_up, w_down)
    return pl.pallas_call(
        body,
        grid=(rows // block,),
        in_specs=[by_rows(joined), by_rows(tokens_all)] + [whole(a) for a in operands[2:]],
        out_specs=by_rows(tokens_all),
        out_shape=jax.ShapeDtypeStruct((rows, width), bf16),
        scratch_shapes=[pltpu.VMEM((block, width), bf16)],
        compiler_params=pltpu.CompilerParams(
            dimension_semantics=("arbitrary",), vmem_limit_bytes=58 * 1024 * 1024
        ),
        cost_estimate=pl.CostEstimate(
            flops=13_000_000_000, bytes_accessed=25_000_000, transcendentals=720_000
        ),
        name="shared",
    )(*operands)


def at_row(start, block):
    return start if isinstance(start, int) else pl.multiple_of(start, block)


def run_experts(x, weights, block=256):
    rows, width = x.shape
    hidden = weights[0].shape[0]
    blocks = rows // block

    def body(x_hbm, g0, u0, d0, g1, u1, d1, out_hbm, xs, outs, gs, us, ds, x_sems, w_sems, out_sems):
        def load_x(i):
            at = pl.ds(at_row(i * block, block), block)
            return pltpu.make_async_copy(x_hbm.at[at], xs.at[at], x_sems.at[i])

        def save(i):
            at = pl.ds(at_row(i * block, block), block)
            return pltpu.make_async_copy(outs.at[at], out_hbm.at[at], out_sems.at[i])

        loads = []
        for half, (g, u, d) in enumerate(((g0, u0, d0), (g1, u1, d1))):
            loads.append(
                (
                    pltpu.make_async_copy(g, gs.at[half], w_sems.at[half, 0]),
                    pltpu.make_async_copy(u, us.at[half], w_sems.at[half, 1]),
                    pltpu.make_async_copy(d, ds.at[half], w_sems.at[half, 2]),
                )
            )
        load_x(0).start()
        for one in loads[0]:
            one.start()
        for i in range(1, blocks):
            load_x(i).start()
        for one in loads[1]:
            one.start()
        across = (((1,), (1,)), ((), ()))
        for half in range(2):

            def step(i, carry, waits):
                at = pl.ds(at_row(i * block, block), block)
                if half == 0:
                    load_x(i).wait()
                if waits:
                    loads[half][0].wait()
                xb = xs[at, :]
                gate = lax.dot_general(xb, gs[half], across, preferred_element_type=f32)
                if waits:
                    loads[half][1].wait()
                up = lax.dot_general(xb, us[half], across, preferred_element_type=f32)
                act = (gate * (1.0 / (1.0 + jnp.exp(-gate))) * up).astype(bf16)
                if waits:
                    loads[half][2].wait()
                res = jnp.dot(act, ds[half], preferred_element_type=f32).astype(bf16)
                if half == 0:
                    outs[at, :] = res
                else:
                    outs[at, :] = (outs[at, :].astype(f32) + res.astype(f32)).astype(bf16)
                    save(i).start()
                return carry

            step(0, 0, True)
            lax.fori_loop(1, blocks, lambda i, carry: step(i, carry, False), 0)
        for i in range(blocks):
            save(i).wait()

    hbm = pl.BlockSpec(memory_space=pl.ANY)
    return pl.pallas_call(
        body,
        in_specs=[hbm] * 7,
        out_specs=hbm,
        out_shape=jax.ShapeDtypeStruct((rows, width), bf16),
        scratch_shapes=[
            pltpu.VMEM((rows, width), bf16),
            pltpu.VMEM((rows, width), bf16),
            pltpu.VMEM((2, hidden, width), bf16),
            pltpu.VMEM((2, hidden, width), bf16),
            pltpu.VMEM((2, hidden, width), bf16),
            pltpu.SemaphoreType.DMA((blocks,)),
            pltpu.SemaphoreType.DMA((2, 3)),
            pltpu.SemaphoreType.DMA((blocks,)),
        ],
        compiler_params=pltpu.CompilerParams(vmem_limit_bytes=60 * 1024 * 1024),
        cost_estimate=pl.CostEstimate(
            flops=17_700_000_000, bytes_accessed=30_000_000, transcendentals=1_500_000
        ),
        name="experts",
    )(x, *weights)


def routing_tables(ids, gates, experts=64):
    top, rows = ids.shape
    slots = experts * CAP

    def body(ids_ref, gates_ref, spread_ref, mixing_ref):
        expert = lax.broadcasted_iota(jnp.int32, (experts, rows), 0)
        chosen = jnp.zeros((experts, rows), f32)
        gate_of = jnp.zeros((experts, rows), f32)
        for route in range(top):
            named = ids_ref[route : route + 1, :] == expert
            chosen = jnp.where(named, 1.0, chosen)
            gate_of = jnp.where(named, gates_ref[route : route + 1, :], gate_of)
        line = lax.broadcasted_iota(jnp.int32, (rows, rows), 0)
        before = (line < lax.broadcasted_iota(jnp.int32, (rows, rows), 1)).astype(f32).astype(bf16)
        earlier = jnp.dot(chosen.astype(bf16), before, preferred_element_type=f32)
        slot = jnp.where(chosen > 0.0, earlier, -1.0)

        owner = lax.broadcasted_iota(jnp.int32, (slots, experts), 0) // CAP
        owned = owner == lax.broadcasted_iota(jnp.int32, (slots, experts), 1)
        repeat = owned.astype(f32).astype(bf16)
        number = (lax.broadcasted_iota(jnp.int32, (slots, rows), 0) % CAP).astype(f32)
        tall = jnp.dot(repeat, slot.astype(bf16), preferred_element_type=f32)
        spread_ref[...] = (tall == number).astype(f32).astype(bf16)

        owner = lax.broadcasted_iota(jnp.int32, (experts, slots), 1) // CAP
        owned = owner == lax.broadcasted_iota(jnp.int32, (experts, slots), 0)
        repeat = owned.astype(f32).astype(bf16)
        number = (lax.broadcasted_iota(jnp.int32, (rows, slots), 1) % CAP).astype(f32)
        wide = jnp.dot(slot.T.astype(bf16), repeat, preferred_element_type=f32)
        hit = wide == number
        rest = gate_of.T
        for part in range(3):
            now = rest.astype(bf16)
            rest = rest - now.astype(f32)
            weights = jnp.dot(now, repeat, preferred_element_type=f32)
            mixing_ref[part * rows : (part + 1) * rows, :] = jnp.where(hit, weights, 0.0).astype(bf16)

    return pl.pallas_call(
        body,
        out_shape=[
            jax.ShapeDtypeStruct((slots, rows), bf16),
            jax.ShapeDtypeStruct((3 * rows, slots), bf16),
        ],
        name="routing",
    )(ids, gates)


def shards(
    tokens,
    position_of_row,
    request_of_position,
    expert_ids,
    gate_values,
    attn_norm,
    moe_norm,
    w_query,
    w_latent,
    w_key_up,
    w_value_up,
    w_output,
    w_shared_gate,
    w_shared_up,
    w_shared_down,
    w_routed_gate,
    w_routed_up,
    w_routed_down,
):
    own = tokens[0]
    rows, width = own.shape
    here = place_of(0, 0)
    core = lax.axis_index("c")

    spread, mixing = routing_tables(expert_ids[0].T, gate_values[0].T)

    span = w_output.shape[1] // 8
    block_here = lax.axis_index("y") * 2 + core
    columns = lax.dynamic_slice(w_output, (0, block_here * span), (w_output.shape[0], span))
    columns = lax.all_gather(columns, SEQ, axis=0, tiled=True)

    early = (spread, mixing, attn_norm.reshape(1, -1), moe_norm.reshape(1, -1))
    tokens_all, (spread, mixing, attn_gain, moe_gain) = gather_rows(own, early)

    own_half = (w_routed_gate[0].T, w_routed_up[0].T, w_routed_down[0])
    columns, own_half, tokens_all = lax.optimization_barrier((columns, own_half, tokens_all))
    other_half = tuple(swap_cores(w) for w in own_half)
    w_out = lax.all_gather(columns, ("y", "c"), axis=0, tiled=False)

    head_out = attention(
        tokens_all,
        attn_gain,
        w_latent,
        w_query,
        w_key_up,
        w_value_up,
        position_of_row,
        request_of_position,
    )
    head_out, other_half = lax.optimization_barrier((head_out, other_half))
    joined = gather_columns(head_out)

    resid, outgoing = run_dispatch(here, joined, own, w_out, moe_gain, spread)
    outgoing, joined = lax.optimization_barrier((outgoing, joined))
    slots = outgoing.shape[0]
    arrived = lax.all_to_all(
        outgoing.reshape(128, slots // 128, width), ALL, split_axis=0, concat_axis=0, tiled=True
    ).reshape(slots, width)

    shared_part = run_shared(
        joined,
        tokens_all,
        w_out,
        moe_gain,
        w_shared_gate.T,
        w_shared_up.T,
        w_shared_down,
    )
    arrived, _ = lax.optimization_barrier((arrived, shared_part))
    shared_out = lax.psum_scatter(
        shared_part,
        SEQ,
        scatter_dimension=0,
        tiled=True,
    )

    expert_out = run_experts(arrived, own_half + other_half)
    returned = lax.all_to_all(
        expert_out.reshape(128, slots // 128, width), ALL, split_axis=0, concat_axis=0, tiled=True
    ).reshape(slots, width)
    layer_out = run_combine(mixing, returned, resid, shared_out)
    return layer_out.reshape(1, rows, width)


def solution(mesh):
    fine = Mesh(mesh.devices.reshape(2, 4, 2, 4, 2), ALL)
    in_specs = (
        P(EXP, SEQ, None),
        P(EXP, None),
        P(EXP, None),
        P(EXP, SEQ, None),
        P(EXP, SEQ, None),
        P(),
        P(),
        P(None, SEQ),
        P(),
        P(None, SEQ),
        P(None, SEQ),
        P(SEQ, None),
        P(None, SEQ),
        P(None, SEQ),
        P(SEQ, None),
        P(ALL, None, None),
        P(ALL, None, None),
        P(ALL, None, None),
    )
    out_specs = P(EXP, SEQ, None)
    return jax.shard_map(shards, mesh=fine, in_specs=in_specs, out_specs=out_specs, check_vma=False)
```

profile of v0, /device:TPU:8, one launch (start us, length us, event | category | flops | bytes accessed | tf_op | source)
XLA Modules:
  0.0 294.1 jit_solution(2222307269704936897)
XLA Ops:
  6.5 1.5 collective-permute-start
  8.0 1.9 collective-permute-start.1
  9.9 2.1 collective-permute-start.2
  12.1 0.7 constant_dynamic-slice_fusion
  12.7 0.0 all-gather.4.cloned.1.call-update
  12.8 0.0 all-gather.6.cloned.1.call-start
  12.9 1.3 copy.24
  14.2 1.3 copy.23
  15.5 1.3 reshape.26.gain_ref
  16.8 1.3 reshape.27.gain_ref
  18.0 1.9 set_down.2
  19.9 2.3 routing.1
  22.2 2.3 collective-permute-start.4
  24.5 0.0 collective-permute-start.5
  24.5 1.5 collective-permute-start.3
  26.0 0.8 constant_dynamic-update-slice_fusion.14
  26.8 0.0 collective-permute-done.2
  26.8 0.8 constant_dynamic-update-slice_fusion.13
  27.6 0.9 constant_dynamic-update-slice_fusion.12
  28.5 14.6 %collective-permute-done.3 = bf16[128,2048]{1,0:T(8,128)(2,1)S(1)} collective-permute-done((bf16[128,2048]{1,0:T(8,128)(2,1)S(1)}, bf16[128,2048]{1,0:T(8,128)(2,1)S(1)}, u32[]{:S(2)}, u32[]{:S(2)}) %collective-permute-start.3) | collective-permute-done | bytes 524320 | tf_op jit(solution)/shard_map/ppermute | solution.py:38
  43.1 0.1 collective-permute-start.6
  43.2 0.0 collective-permute-done.4
  43.3 3.7 %collective-permute-start.7 = (bf16[64,2048]{1,0:T(8,128)(2,1)S(1)}, bf16[64,2048]{1,0:T(8,128)(2,1)S(1)}, u32[]{:S(2)}, u32[]{:S(2)}) collective-permute-start(bf16[64,2048]{1,0:T(8,128)(2,1)S(1)} %slice.17), channel_id=1, source_target_pairs={{0,48},{16,0},{32,16},{48,32},{1,49},{17,1},{33,17},{49,33},{2,50}... | collective-permute-start | bytes 786440 | tf_op jit(solution)/shard_map/ppermute | solution.py:41
  46.9 0.9 constant_dynamic-update-slice_fusion.11
  47.8 0.8 constant_dynamic-update-slice_fusion.10
  48.7 0.9 constant_dynamic-update-slice_fusion.9
  49.5 3.5 %collective-permute-done.6 = bf16[64,2048]{1,0:T(8,128)(2,1)S(1)} collective-permute-done((bf16[64,2048]{1,0:T(8,128)(2,1)S(1)}, bf16[64,2048]{1,0:T(8,128)(2,1)S(1)}, u32[]{:S(2)}, u32[]{:S(2)}) %collective-permute-start.6) | collective-permute-done | bytes 262176 | tf_op jit(solution)/shard_map/ppermute | solution.py:40
  53.0 0.7 constant_dynamic-update-slice_fusion.8
  53.7 0.7 constant_dynamic-update-slice_fusion.7.x_ref
  54.5 0.0 all-gather.6.cloned.1.call-update
  54.5 0.1 collective-permute-start.8
  54.6 0.5 collective-permute-start.9
  55.1 0.1 collective-permute-start.10
  55.2 17.6 %attend.1.own_ref = bf16[1024,256]{1,0:T(8,128)(2,1)} custom-call(bf16[1024,2048]{1,0:T(8,128)(2,1)} %constant_dynamic-update-slice_fusion.7.x_ref, bf16[1,2048]{1,0:T(2,128)(2,1)} %reshape.26.gain_ref, bf16[2048,512]{1,0:T(8,128)(2,1)} %wl_ref.1, bf16[2048,256]{1,0:T(8,128)(2,1)} %wq_ref.1, bf16[512,256]{1,0:T(8,128)(2,1)} %wk_ref.1, ...), custom_call_target="tpu_custom_call" | custom-call | tf_op jit(solution)/shard_map/attend/pallas_call | solution.py:174
  72.8 0.8 collective-permute-start.13
  73.6 0.1 collective-permute-start.11
  73.7 3.1 %collective-permute-start.12 = (bf16[1024,256]{1,0:T(8,128)(2,1)}, bf16[1024,256]{1,0:T(8,128)(2,1)S(1)}, u32[]{:S(2)}, u32[]{:S(2)}) collective-permute-start(bf16[1024,256]{1,0:T(8,128)(2,1)} %attend.1.own_ref), channel_id=1, source_target_pairs={{0,48},{16,0},{32,16},{48,32},{1,49},{17,1},{33,17},{49,33},{2,50}... | collective-permute-start | bytes 1572872 | tf_op jit(solution)/shard_map/ppermute | solution.py:33
  76.8 10.5 %collective-permute-done.13 = bf16[1024,256]{1,0:T(8,128)(2,1)S(1)} collective-permute-done((bf16[1024,256]{1,0:T(8,128)(2,1)}, bf16[1024,256]{1,0:T(8,128)(2,1)S(1)}, u32[]{:S(2)}, u32[]{:S(2)}) %collective-permute-start.13) | collective-permute-done | bytes 524320 | tf_op jit(solution)/shard_map/ppermute | solution.py:34
  87.4 1.8 collective-permute-start.15
  89.1 1.2 collective-permute-start.14
  90.3 1.9 set_down.3
  92.3 0.9 constant_dynamic-update-slice_fusion.6
  93.1 0.9 constant_dynamic-update-slice_fusion.5
  94.0 0.9 constant_dynamic-update-slice_fusion.4
  94.9 6.0 %collective-permute-done.15 = bf16[1024,256]{1,0:T(8,128)(2,1)S(1)} collective-permute-done((bf16[1024,256]{1,0:T(8,128)(2,1)S(1)}, bf16[1024,256]{1,0:T(8,128)(2,1)S(1)}, u32[]{:S(2)}, u32[]{:S(2)}) %collective-permute-start.15) | collective-permute-done | bytes 524320 | tf_op jit(solution)/shard_map/ppermute | solution.py:39
  101.0 3.0 %collective-permute-start.18 = (bf16[512,256]{1,0:T(8,128)(2,1)S(1)}, bf16[512,256]{1,0:T(8,128)(2,1)S(1)}, u32[]{:S(2)}, u32[]{:S(2)}) collective-permute-start(bf16[512,256]{1,0:T(8,128)(2,1)S(1)} %slice.19), channel_id=1, source_target_pairs={{0,48},{16,0},{32,16},{48,32},{1,49},{17,1},{33,17},{49,33},{2,50}... | collective-permute-start | bytes 786440 | tf_op jit(solution)/shard_map/ppermute | solution.py:41
  104.0 0.1 collective-permute-start.17
  104.1 0.9 constant_dynamic-update-slice_fusion.3
  105.0 0.9 constant_dynamic-update-slice_fusion.2
  105.9 0.4 collective-permute-done.16
  106.3 0.9 constant_dynamic-update-slice_fusion.1
  107.2 4.9 %collective-permute-done.17 = bf16[512,256]{1,0:T(8,128)(2,1)S(1)} collective-permute-done((bf16[512,256]{1,0:T(8,128)(2,1)S(1)}, bf16[512,256]{1,0:T(8,128)(2,1)S(1)}, u32[]{:S(2)}, u32[]{:S(2)}) %collective-permute-start.17) | collective-permute-done | bytes 262176 | tf_op jit(solution)/shard_map/ppermute | solution.py:40
  112.1 0.8 constant_dynamic-update-slice_fusion
  112.9 0.7 constant_dynamic-update-slice_fusion.15.j_ref
  113.6 7.8 %dispatch.1 = (bf16[128,2048]{1,0:T(8,128)(2,1)}, bf16[1024,2048]{1,0:T(8,128)(2,1)}) custom-call(s32[1]{0:T(128)} %bitcast.3.place_ref.here_ref, bf16[1024,2048]{1,0:T(8,128)(2,1)} %constant_dynamic-update-slice_fusion.15.j_ref, bf16[128,2048]{1,0:T(8,128)(2,1)} %bitcast.36, bf16[8,2048,256]{2,1,0:T(8,128)(2,1)} %bitcast.28, ...), custom_call_target="tpu_custom_call" | custom-call | tf_op jit(solution)/shard_map/dispatch/pallas_call | solution.py:245
  121.4 7.3 %all-to-all-start = ((bf16[128,8,2048]{2,1,0:T(8,128)(2,1)}), bf16[128,8,2048]{2,1,0:T(8,128)(2,1)}, u32[]{:S(2)}, u32[]{:S(2)}) async-start(bf16[128,8,2048]{2,1,0:T(8,128)(2,1)} %bitcast.30), calls=%async_computation | async-start | bytes 8388608 | tf_op jit(solution)/shard_map/all_to_all | solution.py:534
  128.7 0.3 reduce-scatter.2.cloned.1.call-start
  129.0 23.3 %shared.1 = bf16[1024,2048]{1,0:T(8,128)(2,1)} custom-call(bf16[1024,2048]{1,0:T(8,128)(2,1)} %constant_dynamic-update-slice_fusion.15.j_ref, bf16[1024,2048]{1,0:T(8,128)(2,1)} %constant_dynamic-update-slice_fusion.7.x_ref, bf16[8,2048,256]{2,1,0:T(8,128)(2,1)} %bitcast.29, bf16[1,2048]{1,0:T(2,128)(2,1)} %reshape.27.gain_ref, bf16[352,2048]{1,0:T(8,128)(2,1)} %bitcast.45, ...), custom_call_target="tpu_custom_call" | custom-call | flops 12999999488 | bytes 25000000 | tf_op jit(solution)/shard_map/shared/pallas_call | solution.py:326
  152.3 0.0 reduce-scatter.2.cloned.1.call-update
  152.3 38.7 %all-to-all-done = bf16[128,8,2048]{2,1,0:T(8,128)(2,1)} async-done(((bf16[128,8,2048]{2,1,0:T(8,128)(2,1)}), bf16[128,8,2048]{2,1,0:T(8,128)(2,1)}, u32[]{:S(2)}, u32[]{:S(2)}) %all-to-all-start) | async-done | bytes 4194336 | tf_op jit(solution)/shard_map/all_to_all | solution.py:534
  191.1 27.4 %experts.1 = bf16[1024,2048]{1,0:T(8,128)(2,1)} custom-call(bf16[1024,2048]{1,0:T(8,128)(2,1)} %bitcast.11.x_hbm, bf16[704,2048]{1,0:T(8,128)(2,1)} %bitcast.40, bf16[704,2048]{1,0:T(8,128)(2,1)} %bitcast.42, bf16[704,2048]{1,0:T(8,128)(2,1)} %bitcast.44, bf16[704,2048]{1,0:T(8,128)(2,1)} %collective-permute-done.8.g1, ...), custom_call_target="tpu_custom_call" | custom-call | flops 17699999744 | bytes 30000000 | tf_op jit(solution)/shard_map/experts/pallas_call | solution.py:408
  218.4 0.0 copy-start.1
  218.4 63.7 %all_to_all.10 = bf16[128,8,2048]{2,1,0:T(8,128)(2,1)} all-to-all(bf16[128,8,2048]{2,1,0:T(8,128)(2,1)} %bitcast.31), channel_id=1, replica_groups=mesh['xl'=2,'z'=4,'xh'=2,'y'=4,'c'=2] {'xl','z','xh','y','c'}, dimensions={0} | all-to-all | bytes 8388608 | tf_op jit(solution)/shard_map/all_to_all | solution.py:556
  282.1 5.5 %combine.1 = bf16[128,2048]{1,0:T(8,128)(2,1)} custom-call(bf16[384,1024]{1,0:T(8,128)(2,1)} %get-tuple-element.28.m_ref, bf16[1024,2048]{1,0:T(8,128)(2,1)} %bitcast.27, bf16[128,2048]{1,0:T(8,128)(2,1)} %get-tuple-element.46.resid_ref, bf16[128,2048]{1,0:T(8,128)(2,1)} %reduce-scatter.2.cloned.1.call-done.shared_ref), custom_call_target="tpu_custom_call" | custom-call | tf_op jit(solution)/shard_map/combine/pallas_call | solution.py:286
  (23 shorter events, 0.1 us)
Async XLA Ops:
  6.5 5.5 %copy-start = (bf16[256,2048]{1,0:T(8,128)(2,1)S(1)}, bf16[256,2048]{1,0:T(8,128)(2,1)}, u32[]{:S(2)}) copy-start(bf16[256,2048]{1,0:T(8,128)(2,1)} %param.29) | copy-start | bytes 3145732
  6.5 47.9 %all-gather.4.cloned.1.call-start = ((), (), s32[]{:S(2)}) async-start(), calls=%async_computation.3 | async-start | bytes 1179648 | tf_op jit(solution)/shard_map/all_gather | solution.py:508
  6.5 15.7 %collective-permute-start = (bf16[128,2048]{1,0:T(8,128)(2,1)}, bf16[128,2048]{1,0:T(8,128)(2,1)S(1)}, u32[]{:S(2)}, u32[]{:S(2)}) collective-permute-start(bf16[128,2048]{1,0:T(8,128)(2,1)} %bitcast.32), channel_id=1, source_target_pairs={{0,64},{64,0},{1,65},{65,1},{2,66},{66,2},{3,67},{67,3},{4,68},{68... | collective-permute-start | bytes 1572872 | tf_op jit(solution)/shard_map/ppermute | solution.py:34
  8.0 16.4 %collective-permute-start.1 = (bf16[128,2048]{1,0:T(8,128)(2,1)}, bf16[128,2048]{1,0:T(8,128)(2,1)S(1)}, u32[]{:S(2)}, u32[]{:S(2)}) collective-permute-start(bf16[128,2048]{1,0:T(8,128)(2,1)} %bitcast.33), channel_id=1, source_target_pairs={{0,16},{16,32},{32,48},{48,0},{1,17},{17,33},{33,49},{49,1},{2,18}... | collective-permute-start | bytes 1572872 | tf_op jit(solution)/shard_map/ppermute | solution.py:32
  9.9 16.8 %collective-permute-start.2 = (bf16[128,2048]{1,0:T(8,128)(2,1)}, bf16[128,2048]{1,0:T(8,128)(2,1)S(1)}, u32[]{:S(2)}, u32[]{:S(2)}) collective-permute-start(bf16[128,2048]{1,0:T(8,128)(2,1)} %bitcast.34), channel_id=1, source_target_pairs={{0,48},{16,0},{32,16},{48,32},{1,49},{17,1},{33,17},{49,33},{2,50}... | collective-permute-start | bytes 1572872 | tf_op jit(solution)/shard_map/ppermute | solution.py:33
  12.8 100.8 %all-gather.6.cloned.1.call-start = ((), (), s32[]{:S(2)}) async-start(), calls=%async_computation.5 | async-start | bytes 9437184 | tf_op jit(solution)/shard_map/all_gather | solution.py:516
  22.2 21.0 %collective-permute-start.4 = (bf16[128,2048]{1,0:T(8,128)(2,1)S(1)}, bf16[128,2048]{1,0:T(8,128)(2,1)S(1)}, u32[]{:S(2)}, u32[]{:S(2)}) collective-permute-start(bf16[128,2048]{1,0:T(8,128)(2,1)S(1)} %collective-permute-done), channel_id=1, source_target_pairs={{0,48},{16,0},{32,16},{48,32},{1,49},{17,1},{33,17},{49,33},{2,50}... | collective-permute-start | bytes 1572872 | tf_op jit(solution)/shard_map/ppermute | solution.py:39
  24.5 24.2 %collective-permute-start.5 = (bf16[128,2048]{1,0:T(8,128)(2,1)S(1)}, bf16[128,2048]{1,0:T(8,128)(2,1)S(1)}, u32[]{:S(2)}, u32[]{:S(2)}) collective-permute-start(bf16[128,2048]{1,0:T(8,128)(2,1)S(1)} %collective-permute-done.1), channel_id=1, source_target_pairs={{0,16},{16,32},{32,48},{48,0},{1,17},{17,33},{33,49},{49,1},{2,18}... | collective-permute-start | bytes 1572872 | tf_op jit(solution)/shard_map/ppermute | solution.py:37
  24.5 18.7 %collective-permute-start.3 = (bf16[128,2048]{1,0:T(8,128)(2,1)S(1)}, bf16[128,2048]{1,0:T(8,128)(2,1)S(1)}, u32[]{:S(2)}, u32[]{:S(2)}) collective-permute-start(bf16[128,2048]{1,0:T(8,128)(2,1)S(1)} %collective-permute-done.1), channel_id=1, source_target_pairs={{0,64},{64,0},{1,65},{65,1},{2,66},{66,2},{3,67},{67,3},{4,68},{68... | collective-permute-start | bytes 1572872 | tf_op jit(solution)/shard_map/ppermute | solution.py:38
  43.1 9.9 %collective-permute-start.6 = (bf16[64,2048]{1,0:T(8,128)(2,1)S(1)}, bf16[64,2048]{1,0:T(8,128)(2,1)S(1)}, u32[]{:S(2)}, u32[]{:S(2)}) collective-permute-start(bf16[64,2048]{1,0:T(8,128)(2,1)S(1)} %slice.16), channel_id=1, source_target_pairs={{0,16},{16,32},{32,48},{48,0},{1,17},{17,33},{33,49},{49,1},{2,18}... | collective-permute-start | bytes 786440 | tf_op jit(solution)/shard_map/ppermute | solution.py:40
  43.3 10.5 %collective-permute-start.7 = (bf16[64,2048]{1,0:T(8,128)(2,1)S(1)}, bf16[64,2048]{1,0:T(8,128)(2,1)S(1)}, u32[]{:S(2)}, u32[]{:S(2)}) collective-permute-start(bf16[64,2048]{1,0:T(8,128)(2,1)S(1)} %slice.17), channel_id=1, source_target_pairs={{0,48},{16,0},{32,16},{48,32},{1,49},{17,1},{33,17},{49,33},{2,50}... | collective-permute-start | bytes 786440 | tf_op jit(solution)/shard_map/ppermute | solution.py:41
  54.5 18.3 %collective-permute-start.8 = (bf16[704,2048]{1,0:T(8,128)(2,1)}, bf16[704,2048]{1,0:T(8,128)(2,1)}, u32[]{:S(2)}, u32[]{:S(2)}) collective-permute-start(bf16[704,2048]{1,0:T(8,128)(2,1)} %bitcast.39), channel_id=1, source_target_pairs={{0,1},{1,0},{2,3},{3,2},{4,5},{5,4},{6,7},{7,6},{8,9},{9,8},{10,11... | collective-permute-start | bytes 8650760 | tf_op jit(solution)/shard_map/ppermute | solution.py:100
  54.6 18.2 %collective-permute-start.9 = (bf16[704,2048]{1,0:T(8,128)(2,1)}, bf16[704,2048]{1,0:T(8,128)(2,1)}, u32[]{:S(2)}, u32[]{:S(2)}) collective-permute-start(bf16[704,2048]{1,0:T(8,128)(2,1)} %bitcast.41), channel_id=1, source_target_pairs={{0,1},{1,0},{2,3},{3,2},{4,5},{5,4},{6,7},{7,6},{8,9},{9,8},{10,11... | collective-permute-start | bytes 8650760 | tf_op jit(solution)/shard_map/ppermute | solution.py:100
  55.1 17.7 %collective-permute-start.10 = (bf16[704,2048]{1,0:T(8,128)(2,1)}, bf16[704,2048]{1,0:T(8,128)(2,1)}, u32[]{:S(2)}, u32[]{:S(2)}) collective-permute-start(bf16[704,2048]{1,0:T(8,128)(2,1)} %bitcast.43), channel_id=1, source_target_pairs={{0,1},{1,0},{2,3},{3,2},{4,5},{5,4},{6,7},{7,6},{8,9},{9,8},{10,11... | collective-permute-start | bytes 8650760 | tf_op jit(solution)/shard_map/ppermute | solution.py:100
  72.8 14.5 %collective-permute-start.13 = (bf16[1024,256]{1,0:T(8,128)(2,1)}, bf16[1024,256]{1,0:T(8,128)(2,1)S(1)}, u32[]{:S(2)}, u32[]{:S(2)}) collective-permute-start(bf16[1024,256]{1,0:T(8,128)(2,1)} %attend.1.own_ref), channel_id=1, source_target_pairs={{0,64},{64,0},{1,65},{65,1},{2,66},{66,2},{3,67},{67,3},{4,68},{68... | collective-permute-start | bytes 1572872 | tf_op jit(solution)/shard_map/ppermute | solution.py:34
  73.6 15.5 %collective-permute-start.11 = (bf16[1024,256]{1,0:T(8,128)(2,1)}, bf16[1024,256]{1,0:T(8,128)(2,1)S(1)}, u32[]{:S(2)}, u32[]{:S(2)}) collective-permute-start(bf16[1024,256]{1,0:T(8,128)(2,1)} %attend.1.own_ref), channel_id=1, source_target_pairs={{0,16},{16,32},{32,48},{48,0},{1,17},{17,33},{33,49},{49,1},{2,18}... | collective-permute-start | bytes 1572872 | tf_op jit(solution)/shard_map/ppermute | solution.py:32
  73.7 19.5 %collective-permute-start.12 = (bf16[1024,256]{1,0:T(8,128)(2,1)}, bf16[1024,256]{1,0:T(8,128)(2,1)S(1)}, u32[]{:S(2)}, u32[]{:S(2)}) collective-permute-start(bf16[1024,256]{1,0:T(8,128)(2,1)} %attend.1.own_ref), channel_id=1, source_target_pairs={{0,48},{16,0},{32,16},{48,32},{1,49},{17,1},{33,17},{49,33},{2,50}... | collective-permute-start | bytes 1572872 | tf_op jit(solution)/shard_map/ppermute | solution.py:33
  87.4 13.6 %collective-permute-start.15 = (bf16[1024,256]{1,0:T(8,128)(2,1)S(1)}, bf16[1024,256]{1,0:T(8,128)(2,1)S(1)}, u32[]{:S(2)}, u32[]{:S(2)}) collective-permute-start(bf16[1024,256]{1,0:T(8,128)(2,1)S(1)} %collective-permute-done.13), channel_id=1, source_target_pairs={{0,48},{16,0},{32,16},{48,32},{1,49},{17,1},{33,17},{49,33},{2,50}... | collective-permute-start | bytes 1572872 | tf_op jit(solution)/shard_map/ppermute | solution.py:39
  89.1 14.9 %collective-permute-start.14 = (bf16[1024,256]{1,0:T(8,128)(2,1)S(1)}, bf16[1024,256]{1,0:T(8,128)(2,1)S(1)}, u32[]{:S(2)}, u32[]{:S(2)}) collective-permute-start(bf16[1024,256]{1,0:T(8,128)(2,1)S(1)} %collective-permute-done.11), channel_id=1, source_target_pairs={{0,64},{64,0},{1,65},{65,1},{2,66},{66,2},{3,67},{67,3},{4,68},{68... | collective-permute-start | bytes 1572872 | tf_op jit(solution)/shard_map/ppermute | solution.py:38
  92.3 14.1 %collective-permute-start.16 = (bf16[1024,256]{1,0:T(8,128)(2,1)S(1)}, bf16[1024,256]{1,0:T(8,128)(2,1)S(1)}, u32[]{:S(2)}, u32[]{:S(2)}) collective-permute-start(bf16[1024,256]{1,0:T(8,128)(2,1)S(1)} %collective-permute-done.11), channel_id=1, source_target_pairs={{0,16},{16,32},{32,48},{48,0},{1,17},{17,33},{33,49},{49,1},{2,18}... | collective-permute-start | bytes 1572872 | tf_op jit(solution)/shard_map/ppermute | solution.py:37
  101.0 11.9 %collective-permute-start.18 = (bf16[512,256]{1,0:T(8,128)(2,1)S(1)}, bf16[512,256]{1,0:T(8,128)(2,1)S(1)}, u32[]{:S(2)}, u32[]{:S(2)}) collective-permute-start(bf16[512,256]{1,0:T(8,128)(2,1)S(1)} %slice.19), channel_id=1, source_target_pairs={{0,48},{16,0},{32,16},{48,32},{1,49},{17,1},{33,17},{49,33},{2,50}... | collective-permute-start | bytes 786440 | tf_op jit(solution)/shard_map/ppermute | solution.py:41
  104.0 8.1 %collective-permute-start.17 = (bf16[512,256]{1,0:T(8,128)(2,1)S(1)}, bf16[512,256]{1,0:T(8,128)(2,1)S(1)}, u32[]{:S(2)}, u32[]{:S(2)}) collective-permute-start(bf16[512,256]{1,0:T(8,128)(2,1)S(1)} %slice.18), channel_id=1, source_target_pairs={{0,16},{16,32},{32,48},{48,0},{1,17},{17,33},{33,49},{49,1},{2,18}... | collective-permute-start | bytes 786440 | tf_op jit(solution)/shard_map/ppermute | solution.py:40
  121.4 69.7 %all-to-all-start = ((bf16[128,8,2048]{2,1,0:T(8,128)(2,1)}), bf16[128,8,2048]{2,1,0:T(8,128)(2,1)}, u32[]{:S(2)}, u32[]{:S(2)}) async-start(bf16[128,8,2048]{2,1,0:T(8,128)(2,1)} %bitcast.30), calls=%async_computation | async-start | bytes 8388608 | tf_op jit(solution)/shard_map/all_to_all | solution.py:534
  128.7 153.4 %reduce-scatter.2.cloned.1.call-start = ((), (), s32[]{:S(2)}) async-start(), calls=%async_computation.4 | async-start | bytes 4718592 | tf_op jit(solution)/shard_map/reduce_scatter | solution.py:548
  218.4 69.1 %copy-start.1 = (bf16[256,2048]{1,0:T(8,128)(2,1)S(1)}, bf16[256,2048]{1,0:T(8,128)(2,1)}, u32[]{:S(2)}) copy-start(bf16[256,2048]{1,0:T(8,128)(2,1)} %param.29) | copy-start | bytes 3145732
Sparse Core Ops, SparseCore 0:
  12.9 39.7 all-gather.3
  54.6 48.8 all-gather.5
  152.4 69.0 reduce-scatter.1
where the time goes:
time: 296 us; the launch traced here: 294 us
  Pallas kernels  87.6 us (30%)
  waiting for transfers between devices  78.9 us (27%)
  blocking collectives  63.7 us (22%)
  starting transfers between devices  31.4 us (11%)
  local copies, waits for them, and re-layouts  19.2 us (6%)
  between operations  13.3 us (4%)
    all_to_all x1, blocking collectives, shards(): lax.all_to_all(expert_out.reshape(128, slots // 128, width), ALL, split_a...  63.7 us
    all_to_all x1, waiting for transfers between devices, shards(): lax.all_to_all(outgoing.reshape(128, slots // 128, width), ALL, split_axi...  38.7 us
    pallas_call x1, Pallas kernels, run_experts(): pl.pallas_call(body, in_specs=[hbm] * 7, out_specs=hbm, out_shape=jax.Sha...  27.4 us
    pallas_call x1, Pallas kernels, run_shared(): pl.pallas_call(body, grid=(rows // block,), in_specs=[by_rows(joined), by...  23.3 us
    pallas_call x1, Pallas kernels, attention(): pl.pallas_call(body, grid_spec=pl.GridSpec(grid=(2, blocks), in_specs=[pl...  17.6 us
    ppermute x2, waiting for transfers between devices, gather_pieces(): side_below = lax.ppermute(below, 'xl', flip)  14.6 us
    ppermute x2, waiting for transfers between devices, gather_pieces(): side = lax.ppermute(own, 'xl', flip)  10.5 us
    ppermute x2, waiting for transfers between devices, gather_pieces(): side_far_low = lax.ppermute(side_below[:half], 'z', up)  8.39 us
  transfers between devices with their start and end apart: 23, of which 7 were waited for; matrix products, arithmetic and copies ran while one was open for 7% of the time, Pallas kernels for 25%

commit v1 on v0

--- a/solution.py
+++ b/solution.py
@@ -88,12 +88,13 @@
     )(place.reshape(1), own)
 
 
-def gather_columns(own):
+def gather_columns(own, early):
     rows, width = own.shape
     out = set_down(own, place_of(0, 0), 1)
-    for dx, dz, start, piece in gather_pieces(own)[0][1:]:
+    pieces, (early, out) = gather_pieces(own, (early, out))
+    for dx, dz, start, piece in pieces[1:]:
         out = lax.dynamic_update_slice(out, piece, (start, place_of(dx, dz) * width))
-    return out
+    return out, early
 
 
 def swap_cores(values):
@@ -507,8 +508,7 @@
     columns = lax.dynamic_slice(w_output, (0, block_here * span), (w_output.shape[0], span))
     columns = lax.all_gather(columns, SEQ, axis=0, tiled=True)
 
-    early = (spread, mixing, attn_norm.reshape(1, -1), moe_norm.reshape(1, -1))
-    tokens_all, (spread, mixing, attn_gain, moe_gain) = gather_rows(own, early)
+    tokens_all, attn_gain = gather_rows(own, attn_norm.reshape(1, -1))
 
     own_half = (w_routed_gate[0].T, w_routed_up[0].T, w_routed_down[0])
     columns, own_half, tokens_all = lax.optimization_barrier((columns, own_half, tokens_all))
@@ -526,7 +526,8 @@
         request_of_position,
     )
     head_out, other_half = lax.optimization_barrier((head_out, other_half))
-    joined = gather_columns(head_out)
+    early = (spread, mixing, moe_norm.reshape(1, -1))
+    joined, (spread, mixing, moe_gain) = gather_columns(head_out, early)
 
     resid, outgoing = run_dispatch(here, joined, own, w_out, moe_gain, spread)
     outgoing, joined = lax.optimization_barrier((outgoing, joined))

time: 296 us -> 296 us (level)
    ppermute x2, waiting for transfers between devices: 6.05 us -> 13.2 us  [gather_pieces(): side_above = lax.ppermute(side, 'z', down)]
    ppermute x2, waiting for transfers between devices: 0.01 us -> 6.48 us  [gather_pieces(): below = lax.ppermute(own, 'z', up)]
    ppermute x2, waiting for transfers between devices: 10.5 us -> 4.31 us  [gather_pieces(): side = lax.ppermute(own, 'xl', flip)]
    ppermute x2, waiting for transfers between devices: 14.6 us -> 8.76 us  [gather_pieces(): side_below = lax.ppermute(below, 'xl', flip)]
  transfers between devices with their start and end apart: 23 -> 23, of which waited for: 7 -> 7; matrix products, arithmetic and copies ran while one was open for 7% -> 6% of each run, Pallas kernels for 25% -> 25%
where the time goes in v1:
time: 296 us; the launch traced here: 295 us
  Pallas kernels  87.6 us (30%)
  waiting for transfers between devices  79.8 us (27%)
  blocking collectives  63.7 us (22%)
  starting transfers between devices  33.3 us (11%)
  local copies, waits for them, and re-layouts  17.3 us (6%)
  between operations  13.4 us (5%)
    all_to_all x1, blocking collectives, shards(): lax.all_to_all(expert_out.reshape(128, slots // 128, width), ALL, split_a...  63.7 us
    all_to_all x1, waiting for transfers between devices, shards(): lax.all_to_all(outgoing.reshape(128, slots // 128, width), ALL, split_axi...  38.7 us
    pallas_call x1, Pallas kernels, run_experts(): pl.pallas_call(body, in_specs=[hbm] * 7, out_specs=hbm, out_shape=jax.Sha...  27.4 us
    pallas_call x1, Pallas kernels, run_shared(): pl.pallas_call(body, grid=(rows // block,), in_specs=[by_rows(joined), by...  23.3 us
    pallas_call x1, Pallas kernels, attention(): pl.pallas_call(body, grid_spec=pl.GridSpec(grid=(2, blocks), in_specs=[pl...  17.6 us
    ppermute x2, waiting for transfers between devices, gather_pieces(): side_above = lax.ppermute(side, 'z', down)  13.2 us
    ppermute x2, waiting for transfers between devices, gather_pieces(): side_below = lax.ppermute(below, 'xl', flip)  8.76 us
    all_to_all x1, starting transfers between devices, shards(): lax.all_to_all(outgoing.reshape(128, slots // 128, width), ALL, split_axi...  8.67 us
  transfers between devices with their start and end apart: 23, of which 7 were waited for; matrix products, arithmetic and copies ran while one was open for 6% of the time, Pallas kernels for 25%

profile of v1, /device:TPU:8, one launch (start us, length us, event | category | flops | bytes accessed | tf_op | source)
XLA Modules:
  0.0 294.9 jit_solution(15066394303054037033)
XLA Ops:
  6.5 1.5 collective-permute-start.2
  8.0 1.9 collective-permute-start
  9.9 2.1 collective-permute-start.1
  12.1 0.7 constant_dynamic-slice_fusion
  12.7 0.0 all-gather.4.cloned.1.call-update
  12.8 0.0 all-gather.6.cloned.1.call-start
  12.9 1.3 reshape.27.gain_ref
  14.2 1.9 set_down.2
  16.1 4.3 %collective-permute-done.2 = bf16[128,2048]{1,0:T(8,128)(2,1)S(1)} collective-permute-done((bf16[128,2048]{1,0:T(8,128)(2,1)}, bf16[128,2048]{1,0:T(8,128)(2,1)S(1)}, u32[]{:S(2)}, u32[]{:S(2)}) %collective-permute-start.2) | collective-permute-done | bytes 524320 | tf_op jit(solution)/shard_map/ppermute | solution.py:34
  20.4 4.0 %collective-permute-start.4 = (bf16[128,2048]{1,0:T(8,128)(2,1)S(1)}, bf16[128,2048]{1,0:T(8,128)(2,1)S(1)}, u32[]{:S(2)}, u32[]{:S(2)}) collective-permute-start(bf16[128,2048]{1,0:T(8,128)(2,1)S(1)} %collective-permute-done.2), channel_id=1, source_target_pairs={{0,48},{16,0},{32,16},{48,32},{1,49},{17,1},{33,17},{49,33},{2,50}... | collective-permute-start | bytes 1572872 | tf_op jit(solution)/shard_map/ppermute | solution.py:39
  24.5 1.5 collective-permute-start.3
  26.0 0.8 constant_dynamic-update-slice_fusion.14
  26.8 0.9 constant_dynamic-update-slice_fusion.13
  27.6 0.8 constant_dynamic-update-slice_fusion.12
  28.5 13.2 %collective-permute-done.4 = bf16[128,2048]{1,0:T(8,128)(2,1)S(1)} collective-permute-done((bf16[128,2048]{1,0:T(8,128)(2,1)S(1)}, bf16[128,2048]{1,0:T(8,128)(2,1)S(1)}, u32[]{:S(2)}, u32[]{:S(2)}) %collective-permute-start.4) | collective-permute-done | bytes 524320 | tf_op jit(solution)/shard_map/ppermute | solution.py:39
  41.7 3.8 %collective-permute-start.7 = (bf16[64,2048]{1,0:T(8,128)(2,1)S(1)}, bf16[64,2048]{1,0:T(8,128)(2,1)S(1)}, u32[]{:S(2)}, u32[]{:S(2)}) collective-permute-start(bf16[64,2048]{1,0:T(8,128)(2,1)S(1)} %slice.17), channel_id=1, source_target_pairs={{0,48},{16,0},{32,16},{48,32},{1,49},{17,1},{33,17},{49,33},{2,50}... | collective-permute-start | bytes 786440 | tf_op jit(solution)/shard_map/ppermute | solution.py:41
  45.5 0.1 collective-permute-start.6
  45.6 0.9 constant_dynamic-update-slice_fusion.11
  46.5 0.8 constant_dynamic-update-slice_fusion.10
  47.3 0.8 constant_dynamic-update-slice_fusion.9
  48.2 5.9 %collective-permute-done.6 = bf16[64,2048]{1,0:T(8,128)(2,1)S(1)} collective-permute-done((bf16[64,2048]{1,0:T(8,128)(2,1)S(1)}, bf16[64,2048]{1,0:T(8,128)(2,1)S(1)}, u32[]{:S(2)}, u32[]{:S(2)}) %collective-permute-start.6) | collective-permute-done | bytes 262176 | tf_op jit(solution)/shard_map/ppermute | solution.py:40
  54.1 0.7 constant_dynamic-update-slice_fusion.8
  54.8 0.8 constant_dynamic-update-slice_fusion.7.x_ref
  55.6 0.0 all-gather.6.cloned.1.call-update
  55.6 0.0 copy-start.3
  55.6 0.0 copy-start.4
  55.6 0.0 copy-start.2
  55.6 0.1 collective-permute-start.8
  55.7 0.5 collective-permute-start.9
  56.2 0.1 collective-permute-start.10
  56.3 17.6 %attend.1.own_ref = bf16[1024,256]{1,0:T(8,128)(2,1)} custom-call(bf16[1024,2048]{1,0:T(8,128)(2,1)} %constant_dynamic-update-slice_fusion.7.x_ref, bf16[1,2048]{1,0:T(2,128)(2,1)} %reshape.27.gain_ref, bf16[2048,512]{1,0:T(8,128)(2,1)} %wl_ref.1, bf16[2048,256]{1,0:T(8,128)(2,1)} %wq_ref.1, bf16[512,256]{1,0:T(8,128)(2,1)} %wk_ref.1, ...), custom_call_target="tpu_custom_call" | custom-call | tf_op jit(solution)/shard_map/attend/pallas_call | solution.py:175
  73.9 0.1 collective-permute-start.12
  74.0 0.1 collective-permute-start.11
  74.1 3.1 %collective-permute-start.13 = (bf16[1024,256]{1,0:T(8,128)(2,1)}, bf16[1024,256]{1,0:T(8,128)(2,1)S(1)}, u32[]{:S(2)}, u32[]{:S(2)}) collective-permute-start(bf16[1024,256]{1,0:T(8,128)(2,1)} %attend.1.own_ref), channel_id=1, source_target_pairs={{0,48},{16,0},{32,16},{48,32},{1,49},{17,1},{33,17},{49,33},{2,50}... | collective-permute-start | bytes 1572872 | tf_op jit(solution)/shard_map/ppermute | solution.py:33
  77.3 0.6 copy.24
  77.8 0.6 copy.23
  78.4 0.6 reshape.28.gain_ref
  79.0 2.3 routing.1
  81.3 1.9 set_down.3
  83.2 6.5 %collective-permute-done.12 = bf16[1024,256]{1,0:T(8,128)(2,1)S(1)} collective-permute-done((bf16[1024,256]{1,0:T(8,128)(2,1)}, bf16[1024,256]{1,0:T(8,128)(2,1)S(1)}, u32[]{:S(2)}, u32[]{:S(2)}) %collective-permute-start.12) | collective-permute-done | bytes 524320 | tf_op jit(solution)/shard_map/ppermute | solution.py:32
  89.7 1.7 collective-permute-start.15
  91.4 0.3 collective-permute-start.16
  91.7 0.9 constant_dynamic-update-slice_fusion.6
  92.6 0.9 constant_dynamic-update-slice_fusion.5
  93.5 0.9 constant_dynamic-update-slice_fusion.4
  94.4 8.8 %collective-permute-done.14 = bf16[1024,256]{1,0:T(8,128)(2,1)S(1)} collective-permute-done((bf16[1024,256]{1,0:T(8,128)(2,1)S(1)}, bf16[1024,256]{1,0:T(8,128)(2,1)S(1)}, u32[]{:S(2)}, u32[]{:S(2)}) %collective-permute-start.14) | collective-permute-done | bytes 524320 | tf_op jit(solution)/shard_map/ppermute | solution.py:38
  103.2 0.1 collective-permute-start.17
  103.3 3.3 %collective-permute-start.18 = (bf16[512,256]{1,0:T(8,128)(2,1)S(1)}, bf16[512,256]{1,0:T(8,128)(2,1)S(1)}, u32[]{:S(2)}, u32[]{:S(2)}) collective-permute-start(bf16[512,256]{1,0:T(8,128)(2,1)S(1)} %slice.19), channel_id=1, source_target_pairs={{0,48},{16,0},{32,16},{48,32},{1,49},{17,1},{33,17},{49,33},{2,50}... | collective-permute-start | bytes 786440 | tf_op jit(solution)/shard_map/ppermute | solution.py:41
  106.6 0.9 constant_dynamic-update-slice_fusion.3
  107.5 0.9 constant_dynamic-update-slice_fusion.2
  108.4 0.9 constant_dynamic-update-slice_fusion.1
  109.2 2.3 collective-permute-done.17
  111.5 0.8 constant_dynamic-update-slice_fusion
  112.3 0.7 constant_dynamic-update-slice_fusion.15.j_ref
  113.0 7.8 %dispatch.1 = (bf16[128,2048]{1,0:T(8,128)(2,1)}, bf16[1024,2048]{1,0:T(8,128)(2,1)}) custom-call(s32[1]{0:T(128)} %bitcast.5.place_ref.here_ref, bf16[1024,2048]{1,0:T(8,128)(2,1)} %constant_dynamic-update-slice_fusion.15.j_ref, bf16[128,2048]{1,0:T(8,128)(2,1)} %bitcast.36, bf16[8,2048,256]{2,1,0:T(8,128)(2,1)} %bitcast.28, ...), custom_call_target="tpu_custom_call" | custom-call | tf_op jit(solution)/shard_map/dispatch/pallas_call | solution.py:246
  120.8 8.7 %all-to-all-start = ((bf16[128,8,2048]{2,1,0:T(8,128)(2,1)}), bf16[128,8,2048]{2,1,0:T(8,128)(2,1)}, u32[]{:S(2)}, u32[]{:S(2)}) async-start(bf16[128,8,2048]{2,1,0:T(8,128)(2,1)} %bitcast.30), calls=%async_computation | async-start | bytes 8388608 | tf_op jit(solution)/shard_map/all_to_all | solution.py:535
  129.5 0.3 reduce-scatter.2.cloned.1.call-start
  129.7 23.3 %shared.1 = bf16[1024,2048]{1,0:T(8,128)(2,1)} custom-call(bf16[1024,2048]{1,0:T(8,128)(2,1)} %constant_dynamic-update-slice_fusion.15.j_ref, bf16[1024,2048]{1,0:T(8,128)(2,1)} %constant_dynamic-update-slice_fusion.7.x_ref, bf16[8,2048,256]{2,1,0:T(8,128)(2,1)} %bitcast.29, bf16[1,2048]{1,0:T(2,128)(2,1)} %reshape.28.gain_ref, bf16[352,2048]{1,0:T(8,128)(2,1)} %bitcast.45, ...), custom_call_target="tpu_custom_call" | custom-call | flops 12999999488 | bytes 25000000 | tf_op jit(solution)/shard_map/shared/pallas_call | solution.py:327
  153.1 0.0 reduce-scatter.2.cloned.1.call-update
  153.1 38.7 %all-to-all-done = bf16[128,8,2048]{2,1,0:T(8,128)(2,1)} async-done(((bf16[128,8,2048]{2,1,0:T(8,128)(2,1)}), bf16[128,8,2048]{2,1,0:T(8,128)(2,1)}, u32[]{:S(2)}, u32[]{:S(2)}) %all-to-all-start) | async-done | bytes 4194336 | tf_op jit(solution)/shard_map/all_to_all | solution.py:535
  191.8 27.4 %experts.1 = bf16[1024,2048]{1,0:T(8,128)(2,1)} custom-call(bf16[1024,2048]{1,0:T(8,128)(2,1)} %bitcast.11.x_hbm, bf16[704,2048]{1,0:T(8,128)(2,1)} %bitcast.40, bf16[704,2048]{1,0:T(8,128)(2,1)} %bitcast.42, bf16[704,2048]{1,0:T(8,128)(2,1)} %bitcast.44, bf16[704,2048]{1,0:T(8,128)(2,1)} %collective-permute-done.8.g1, ...), custom_call_target="tpu_custom_call" | custom-call | flops 17699999744 | bytes 30000000 | tf_op jit(solution)/shard_map/experts/pallas_call | solution.py:409
  219.2 0.0 copy-start.1
  219.2 63.7 %all_to_all.10 = bf16[128,8,2048]{2,1,0:T(8,128)(2,1)} all-to-all(bf16[128,8,2048]{2,1,0:T(8,128)(2,1)} %bitcast.31), channel_id=1, replica_groups=mesh['xl'=2,'z'=4,'xh'=2,'y'=4,'c'=2] {'xl','z','xh','y','c'}, dimensions={0} | all-to-all | bytes 8388608 | tf_op jit(solution)/shard_map/all_to_all | solution.py:557
  282.9 5.5 %combine.1 = bf16[128,2048]{1,0:T(8,128)(2,1)} custom-call(bf16[384,1024]{1,0:T(8,128)(2,1)} %get-tuple-element.37.m_ref, bf16[1024,2048]{1,0:T(8,128)(2,1)} %bitcast.27, bf16[128,2048]{1,0:T(8,128)(2,1)} %get-tuple-element.50.resid_ref, bf16[128,2048]{1,0:T(8,128)(2,1)} %reduce-scatter.2.cloned.1.call-done.shared_ref), custom_call_target="tpu_custom_call" | custom-call | tf_op jit(solution)/shard_map/combine/pallas_call | solution.py:287
  (29 shorter events, 0.1 us)
Async XLA Ops:
  6.5 5.5 %copy-start = (bf16[256,2048]{1,0:T(8,128)(2,1)S(1)}, bf16[256,2048]{1,0:T(8,128)(2,1)}, u32[]{:S(2)}) copy-start(bf16[256,2048]{1,0:T(8,128)(2,1)} %param.29) | copy-start | bytes 3145732
  6.5 49.0 %all-gather.4.cloned.1.call-start = ((), (), s32[]{:S(2)}) async-start(), calls=%async_computation.3 | async-start | bytes 1179648 | tf_op jit(solution)/shard_map/all_gather | solution.py:509
  6.5 13.9 %collective-permute-start.2 = (bf16[128,2048]{1,0:T(8,128)(2,1)}, bf16[128,2048]{1,0:T(8,128)(2,1)S(1)}, u32[]{:S(2)}, u32[]{:S(2)}) collective-permute-start(bf16[128,2048]{1,0:T(8,128)(2,1)} %bitcast.32), channel_id=1, source_target_pairs={{0,64},{64,0},{1,65},{65,1},{2,66},{66,2},{3,67},{67,3},{4,68},{68... | collective-permute-start | bytes 1572872 | tf_op jit(solution)/shard_map/ppermute | solution.py:34
  8.0 16.4 %collective-permute-start = (bf16[128,2048]{1,0:T(8,128)(2,1)}, bf16[128,2048]{1,0:T(8,128)(2,1)S(1)}, u32[]{:S(2)}, u32[]{:S(2)}) collective-permute-start(bf16[128,2048]{1,0:T(8,128)(2,1)} %bitcast.33), channel_id=1, source_target_pairs={{0,16},{16,32},{32,48},{48,0},{1,17},{17,33},{33,49},{49,1},{2,18}... | collective-permute-start | bytes 1572872 | tf_op jit(solution)/shard_map/ppermute | solution.py:32
  9.9 16.8 %collective-permute-start.1 = (bf16[128,2048]{1,0:T(8,128)(2,1)}, bf16[128,2048]{1,0:T(8,128)(2,1)S(1)}, u32[]{:S(2)}, u32[]{:S(2)}) collective-permute-start(bf16[128,2048]{1,0:T(8,128)(2,1)} %bitcast.34), channel_id=1, source_target_pairs={{0,48},{16,0},{32,16},{48,32},{1,49},{17,1},{33,17},{49,33},{2,50}... | collective-permute-start | bytes 1572872 | tf_op jit(solution)/shard_map/ppermute | solution.py:33
  12.8 100.3 %all-gather.6.cloned.1.call-start = ((), (), s32[]{:S(2)}) async-start(), calls=%async_computation.5 | async-start | bytes 9437184 | tf_op jit(solution)/shard_map/all_gather | solution.py:516
  20.4 21.2 %collective-permute-start.4 = (bf16[128,2048]{1,0:T(8,128)(2,1)S(1)}, bf16[128,2048]{1,0:T(8,128)(2,1)S(1)}, u32[]{:S(2)}, u32[]{:S(2)}) collective-permute-start(bf16[128,2048]{1,0:T(8,128)(2,1)S(1)} %collective-permute-done.2), channel_id=1, source_target_pairs={{0,48},{16,0},{32,16},{48,32},{1,49},{17,1},{33,17},{49,33},{2,50}... | collective-permute-start | bytes 1572872 | tf_op jit(solution)/shard_map/ppermute | solution.py:39
  24.5 22.9 %collective-permute-start.5 = (bf16[128,2048]{1,0:T(8,128)(2,1)S(1)}, bf16[128,2048]{1,0:T(8,128)(2,1)S(1)}, u32[]{:S(2)}, u32[]{:S(2)}) collective-permute-start(bf16[128,2048]{1,0:T(8,128)(2,1)S(1)} %collective-permute-done), channel_id=1, source_target_pairs={{0,16},{16,32},{32,48},{48,0},{1,17},{17,33},{33,49},{49,1},{2,18}... | collective-permute-start | bytes 1572872 | tf_op jit(solution)/shard_map/ppermute | solution.py:37
  24.5 21.0 %collective-permute-start.3 = (bf16[128,2048]{1,0:T(8,128)(2,1)S(1)}, bf16[128,2048]{1,0:T(8,128)(2,1)S(1)}, u32[]{:S(2)}, u32[]{:S(2)}) collective-permute-start(bf16[128,2048]{1,0:T(8,128)(2,1)S(1)} %collective-permute-done), channel_id=1, source_target_pairs={{0,64},{64,0},{1,65},{65,1},{2,66},{66,2},{3,67},{67,3},{4,68},{68... | collective-permute-start | bytes 1572872 | tf_op jit(solution)/shard_map/ppermute | solution.py:38
  41.7 13.2 %collective-permute-start.7 = (bf16[64,2048]{1,0:T(8,128)(2,1)S(1)}, bf16[64,2048]{1,0:T(8,128)(2,1)S(1)}, u32[]{:S(2)}, u32[]{:S(2)}) collective-permute-start(bf16[64,2048]{1,0:T(8,128)(2,1)S(1)} %slice.17), channel_id=1, source_target_pairs={{0,48},{16,0},{32,16},{48,32},{1,49},{17,1},{33,17},{49,33},{2,50}... | collective-permute-start | bytes 786440 | tf_op jit(solution)/shard_map/ppermute | solution.py:41
  45.5 8.6 %collective-permute-start.6 = (bf16[64,2048]{1,0:T(8,128)(2,1)S(1)}, bf16[64,2048]{1,0:T(8,128)(2,1)S(1)}, u32[]{:S(2)}, u32[]{:S(2)}) collective-permute-start(bf16[64,2048]{1,0:T(8,128)(2,1)S(1)} %slice.16), channel_id=1, source_target_pairs={{0,16},{16,32},{32,48},{48,0},{1,17},{17,33},{33,49},{49,1},{2,18}... | collective-permute-start | bytes 786440 | tf_op jit(solution)/shard_map/ppermute | solution.py:40
  55.6 21.6 %copy-start.3 = (s32[1,128,6]{1,0,2:T(1,128)S(1)}, s32[1,128,6]{1,0,2:T(1,128)}, u32[]{:S(2)}) copy-start(s32[1,128,6]{1,0,2:T(1,128)} %param.21) | copy-start | bytes 9220
  55.6 22.2 %copy-start.4 = (f32[1,128,6]{1,0,2:T(1,128)S(1)}, f32[1,128,6]{1,0,2:T(1,128)}, u32[]{:S(2)}) copy-start(f32[1,128,6]{1,0,2:T(1,128)} %param.22) | copy-start | bytes 9220
  55.6 22.8 %copy-start.2 = (bf16[2048]{0:T(1024)(128)(2,1)S(1)}, bf16[2048]{0:T(1024)(128)(2,1)}, u32[]{:S(2)}) copy-start(bf16[2048]{0:T(1024)(128)(2,1)} %param.24) | copy-start | bytes 12292
  55.6 18.3 %collective-permute-start.8 = (bf16[704,2048]{1,0:T(8,128)(2,1)}, bf16[704,2048]{1,0:T(8,128)(2,1)}, u32[]{:S(2)}, u32[]{:S(2)}) collective-permute-start(bf16[704,2048]{1,0:T(8,128)(2,1)} %bitcast.39), channel_id=1, source_target_pairs={{0,1},{1,0},{2,3},{3,2},{4,5},{5,4},{6,7},{7,6},{8,9},{9,8},{10,11... | collective-permute-start | bytes 8650760 | tf_op jit(solution)/shard_map/ppermute | solution.py:101
  55.7 18.2 %collective-permute-start.9 = (bf16[704,2048]{1,0:T(8,128)(2,1)}, bf16[704,2048]{1,0:T(8,128)(2,1)}, u32[]{:S(2)}, u32[]{:S(2)}) collective-permute-start(bf16[704,2048]{1,0:T(8,128)(2,1)} %bitcast.41), channel_id=1, source_target_pairs={{0,1},{1,0},{2,3},{3,2},{4,5},{5,4},{6,7},{7,6},{8,9},{9,8},{10,11... | collective-permute-start | bytes 8650760 | tf_op jit(solution)/shard_map/ppermute | solution.py:101
  56.2 17.7 %collective-permute-start.10 = (bf16[704,2048]{1,0:T(8,128)(2,1)}, bf16[704,2048]{1,0:T(8,128)(2,1)}, u32[]{:S(2)}, u32[]{:S(2)}) collective-permute-start(bf16[704,2048]{1,0:T(8,128)(2,1)} %bitcast.43), channel_id=1, source_target_pairs={{0,1},{1,0},{2,3},{3,2},{4,5},{5,4},{6,7},{7,6},{8,9},{9,8},{10,11... | collective-permute-start | bytes 8650760 | tf_op jit(solution)/shard_map/ppermute | solution.py:101
  73.9 15.8 %collective-permute-start.12 = (bf16[1024,256]{1,0:T(8,128)(2,1)}, bf16[1024,256]{1,0:T(8,128)(2,1)S(1)}, u32[]{:S(2)}, u32[]{:S(2)}) collective-permute-start(bf16[1024,256]{1,0:T(8,128)(2,1)} %attend.1.own_ref), channel_id=1, source_target_pairs={{0,16},{16,32},{32,48},{48,0},{1,17},{17,33},{33,49},{49,1},{2,18}... | collective-permute-start | bytes 1572872 | tf_op jit(solution)/shard_map/ppermute | solution.py:32
  74.0 15.7 %collective-permute-start.11 = (bf16[1024,256]{1,0:T(8,128)(2,1)}, bf16[1024,256]{1,0:T(8,128)(2,1)S(1)}, u32[]{:S(2)}, u32[]{:S(2)}) collective-permute-start(bf16[1024,256]{1,0:T(8,128)(2,1)} %attend.1.own_ref), channel_id=1, source_target_pairs={{0,64},{64,0},{1,65},{65,1},{2,66},{66,2},{3,67},{67,3},{4,68},{68... | collective-permute-start | bytes 1572872 | tf_op jit(solution)/shard_map/ppermute | solution.py:34
  74.1 18.5 %collective-permute-start.13 = (bf16[1024,256]{1,0:T(8,128)(2,1)}, bf16[1024,256]{1,0:T(8,128)(2,1)S(1)}, u32[]{:S(2)}, u32[]{:S(2)}) collective-permute-start(bf16[1024,256]{1,0:T(8,128)(2,1)} %attend.1.own_ref), channel_id=1, source_target_pairs={{0,48},{16,0},{32,16},{48,32},{1,49},{17,1},{33,17},{49,33},{2,50}... | collective-permute-start | bytes 1572872 | tf_op jit(solution)/shard_map/ppermute | solution.py:33
  89.7 13.5 %collective-permute-start.14 = (bf16[1024,256]{1,0:T(8,128)(2,1)S(1)}, bf16[1024,256]{1,0:T(8,128)(2,1)S(1)}, u32[]{:S(2)}, u32[]{:S(2)}) collective-permute-start(bf16[1024,256]{1,0:T(8,128)(2,1)S(1)} %collective-permute-done.12), channel_id=1, source_target_pairs={{0,64},{64,0},{1,65},{65,1},{2,66},{66,2},{3,67},{67,3},{4,68},{68... | collective-permute-start | bytes 1572872 | tf_op jit(solution)/shard_map/ppermute | solution.py:38
  89.7 13.6 %collective-permute-start.15 = (bf16[1024,256]{1,0:T(8,128)(2,1)S(1)}, bf16[1024,256]{1,0:T(8,128)(2,1)S(1)}, u32[]{:S(2)}, u32[]{:S(2)}) collective-permute-start(bf16[1024,256]{1,0:T(8,128)(2,1)S(1)} %collective-permute-done.11), channel_id=1, source_target_pairs={{0,48},{16,0},{32,16},{48,32},{1,49},{17,1},{33,17},{49,33},{2,50}... | collective-permute-start | bytes 1572872 | tf_op jit(solution)/shard_map/ppermute | solution.py:39
  91.4 16.9 %collective-permute-start.16 = (bf16[1024,256]{1,0:T(8,128)(2,1)S(1)}, bf16[1024,256]{1,0:T(8,128)(2,1)S(1)}, u32[]{:S(2)}, u32[]{:S(2)}) collective-permute-start(bf16[1024,256]{1,0:T(8,128)(2,1)S(1)} %collective-permute-done.12), channel_id=1, source_target_pairs={{0,16},{16,32},{32,48},{48,0},{1,17},{17,33},{33,49},{49,1},{2,18}... | collective-permute-start | bytes 1572872 | tf_op jit(solution)/shard_map/ppermute | solution.py:37
  103.2 8.3 %collective-permute-start.17 = (bf16[512,256]{1,0:T(8,128)(2,1)S(1)}, bf16[512,256]{1,0:T(8,128)(2,1)S(1)}, u32[]{:S(2)}, u32[]{:S(2)}) collective-permute-start(bf16[512,256]{1,0:T(8,128)(2,1)S(1)} %slice.18), channel_id=1, source_target_pairs={{0,16},{16,32},{32,48},{48,0},{1,17},{17,33},{33,49},{49,1},{2,18}... | collective-permute-start | bytes 786440 | tf_op jit(solution)/shard_map/ppermute | solution.py:40
  103.3 9.0 %collective-permute-start.18 = (bf16[512,256]{1,0:T(8,128)(2,1)S(1)}, bf16[512,256]{1,0:T(8,128)(2,1)S(1)}, u32[]{:S(2)}, u32[]{:S(2)}) collective-permute-start(bf16[512,256]{1,0:T(8,128)(2,1)S(1)} %slice.19), channel_id=1, source_target_pairs={{0,48},{16,0},{32,16},{48,32},{1,49},{17,1},{33,17},{49,33},{2,50}... | collective-permute-start | bytes 786440 | tf_op jit(solution)/shard_map/ppermute | solution.py:41
  120.8 71.1 %all-to-all-start = ((bf16[128,8,2048]{2,1,0:T(8,128)(2,1)}), bf16[128,8,2048]{2,1,0:T(8,128)(2,1)}, u32[]{:S(2)}, u32[]{:S(2)}) async-start(bf16[128,8,2048]{2,1,0:T(8,128)(2,1)} %bitcast.30), calls=%async_computation | async-start | bytes 8388608 | tf_op jit(solution)/shard_map/all_to_all | solution.py:535
  129.5 153.4 %reduce-scatter.2.cloned.1.call-start = ((), (), s32[]{:S(2)}) async-start(), calls=%async_computation.4 | async-start | bytes 4718592 | tf_op jit(solution)/shard_map/reduce_scatter | solution.py:549
  219.2 69.1 %copy-start.1 = (bf16[256,2048]{1,0:T(8,128)(2,1)S(1)}, bf16[256,2048]{1,0:T(8,128)(2,1)}, u32[]{:S(2)}) copy-start(bf16[256,2048]{1,0:T(8,128)(2,1)} %param.29) | copy-start | bytes 3145732
Sparse Core Ops, SparseCore 0:
  12.9 39.7 all-gather.3
  55.7 47.6 all-gather.5
  153.2 69.0 reduce-scatter.1

commit v2 on v0

--- a/solution.py
+++ b/solution.py
@@ -273,7 +273,7 @@
     )(here.reshape(1), joined, own, w_out, gain, spread)
 
 
-def run_combine(mixing, returned, resid, shared_out, block=512):
+def run_combine(mixing, returned, resid, shared_out, block=1024):
     rows, width = resid.shape
 
     def body(m_ref, r_ref, resid_ref, shared_ref, out_ref):

time: 296 us -> 295 us (level)
  no operation moved by 1% of the time
where the time goes in v2:
time: 295 us; the launch traced here: 294 us
  Pallas kernels  87.5 us (30%)
  waiting for transfers between devices  78.9 us (27%)
  blocking collectives  63.7 us (22%)
  starting transfers between devices  31.4 us (11%)
  local copies, waits for them, and re-layouts  19.2 us (7%)
  between operations  13.3 us (5%)
    all_to_all x1, blocking collectives, shards(): lax.all_to_all(expert_out.reshape(128, slots // 128, width), ALL, split_a...  63.7 us
    all_to_all x1, waiting for transfers between devices, shards(): lax.all_to_all(outgoing.reshape(128, slots // 128, width), ALL, split_axi...  38.7 us
    pallas_call x1, Pallas kernels, run_experts(): pl.pallas_call(body, in_specs=[hbm] * 7, out_specs=hbm, out_shape=jax.Sha...  27.4 us
    pallas_call x1, Pallas kernels, run_shared(): pl.pallas_call(body, grid=(rows // block,), in_specs=[by_rows(joined), by...  23.3 us
    pallas_call x1, Pallas kernels, attention(): pl.pallas_call(body, grid_spec=pl.GridSpec(grid=(2, blocks), in_specs=[pl...  17.6 us
    ppermute x2, waiting for transfers between devices, gather_pieces(): side_below = lax.ppermute(below, 'xl', flip)  14.6 us
    ppermute x2, waiting for transfers between devices, gather_pieces(): side = lax.ppermute(own, 'xl', flip)  10.5 us
    ppermute x2, waiting for transfers between devices, gather_pieces(): side_far_low = lax.ppermute(side_below[:half], 'z', up)  8.39 us
  transfers between devices with their start and end apart: 23, of which 7 were waited for; matrix products, arithmetic and copies ran while one was open for 7% of the time, Pallas kernels for 25%

profile of v2, /device:TPU:8, one launch (start us, length us, event | category | flops | bytes accessed | tf_op | source)
XLA Modules:
  0.0 294.0 jit_solution(14043999013105739295)
XLA Ops:
  6.5 1.5 collective-permute-start
  8.0 1.9 collective-permute-start.1
  9.9 2.1 collective-permute-start.2
  12.1 0.7 constant_dynamic-slice_fusion
  12.7 0.0 all-gather.4.cloned.1.call-update
  12.8 0.0 all-gather.6.cloned.1.call-start
  12.9 1.3 copy.24
  14.2 1.3 copy.23
  15.5 1.3 reshape.26.gain_ref
  16.8 1.3 reshape.27.gain_ref
  18.0 1.9 set_down.2
  19.9 2.3 routing.1
  22.2 0.0 collective-permute-done
  22.2 2.3 collective-permute-start.4
  24.5 0.0 collective-permute-done.1
  24.5 0.0 collective-permute-start.5
  24.5 1.5 collective-permute-start.3
  26.0 0.8 constant_dynamic-update-slice_fusion.14
  26.8 0.8 constant_dynamic-update-slice_fusion.13
  27.6 0.9 constant_dynamic-update-slice_fusion.12
  28.5 14.6 %collective-permute-done.3 = bf16[128,2048]{1,0:T(8,128)(2,1)S(1)} collective-permute-done((bf16[128,2048]{1,0:T(8,128)(2,1)S(1)}, bf16[128,2048]{1,0:T(8,128)(2,1)S(1)}, u32[]{:S(2)}, u32[]{:S(2)}) %collective-permute-start.3) | collective-permute-done | bytes 524320 | tf_op jit(solution)/shard_map/ppermute | solution.py:38
  43.1 0.1 collective-permute-start.6
  43.3 3.7 %collective-permute-start.7 = (bf16[64,2048]{1,0:T(8,128)(2,1)S(1)}, bf16[64,2048]{1,0:T(8,128)(2,1)S(1)}, u32[]{:S(2)}, u32[]{:S(2)}) collective-permute-start(bf16[64,2048]{1,0:T(8,128)(2,1)S(1)} %slice.17), channel_id=1, source_target_pairs={{0,48},{16,0},{32,16},{48,32},{1,49},{17,1},{33,17},{49,33},{2,50}... | collective-permute-start | bytes 786440 | tf_op jit(solution)/shard_map/ppermute | solution.py:41
  46.9 0.9 constant_dynamic-update-slice_fusion.11
  47.8 0.8 constant_dynamic-update-slice_fusion.10
  48.7 0.9 constant_dynamic-update-slice_fusion.9
  49.5 3.5 %collective-permute-done.6 = bf16[64,2048]{1,0:T(8,128)(2,1)S(1)} collective-permute-done((bf16[64,2048]{1,0:T(8,128)(2,1)S(1)}, bf16[64,2048]{1,0:T(8,128)(2,1)S(1)}, u32[]{:S(2)}, u32[]{:S(2)}) %collective-permute-start.6) | collective-permute-done | bytes 262176 | tf_op jit(solution)/shard_map/ppermute | solution.py:40
  53.0 0.7 constant_dynamic-update-slice_fusion.8
  53.7 0.7 constant_dynamic-update-slice_fusion.7.x_ref
  54.5 0.0 all-gather.6.cloned.1.call-update
  54.5 0.1 collective-permute-start.8
  54.6 0.5 collective-permute-start.9
  55.1 0.1 collective-permute-start.10
  55.2 17.6 %attend.1.own_ref = bf16[1024,256]{1,0:T(8,128)(2,1)} custom-call(bf16[1024,2048]{1,0:T(8,128)(2,1)} %constant_dynamic-update-slice_fusion.7.x_ref, bf16[1,2048]{1,0:T(2,128)(2,1)} %reshape.26.gain_ref, bf16[2048,512]{1,0:T(8,128)(2,1)} %wl_ref.1, bf16[2048,256]{1,0:T(8,128)(2,1)} %wq_ref.1, bf16[512,256]{1,0:T(8,128)(2,1)} %wk_ref.1, ...), custom_call_target="tpu_custom_call" | custom-call | tf_op jit(solution)/shard_map/attend/pallas_call | solution.py:174
  72.8 0.8 collective-permute-start.13
  73.6 0.1 collective-permute-start.11
  73.7 3.1 %collective-permute-start.12 = (bf16[1024,256]{1,0:T(8,128)(2,1)}, bf16[1024,256]{1,0:T(8,128)(2,1)S(1)}, u32[]{:S(2)}, u32[]{:S(2)}) collective-permute-start(bf16[1024,256]{1,0:T(8,128)(2,1)} %attend.1.own_ref), channel_id=1, source_target_pairs={{0,48},{16,0},{32,16},{48,32},{1,49},{17,1},{33,17},{49,33},{2,50}... | collective-permute-start | bytes 1572872 | tf_op jit(solution)/shard_map/ppermute | solution.py:33
  76.8 10.5 %collective-permute-done.13 = bf16[1024,256]{1,0:T(8,128)(2,1)S(1)} collective-permute-done((bf16[1024,256]{1,0:T(8,128)(2,1)}, bf16[1024,256]{1,0:T(8,128)(2,1)S(1)}, u32[]{:S(2)}, u32[]{:S(2)}) %collective-permute-start.13) | collective-permute-done | bytes 524320 | tf_op jit(solution)/shard_map/ppermute | solution.py:34
  87.4 1.8 collective-permute-start.15
  89.1 1.2 collective-permute-start.14
  90.3 1.9 set_down.3
  92.3 0.9 constant_dynamic-update-slice_fusion.6
  93.1 0.9 constant_dynamic-update-slice_fusion.5
  94.0 0.9 constant_dynamic-update-slice_fusion.4
  94.9 6.0 %collective-permute-done.15 = bf16[1024,256]{1,0:T(8,128)(2,1)S(1)} collective-permute-done((bf16[1024,256]{1,0:T(8,128)(2,1)S(1)}, bf16[1024,256]{1,0:T(8,128)(2,1)S(1)}, u32[]{:S(2)}, u32[]{:S(2)}) %collective-permute-start.15) | collective-permute-done | bytes 524320 | tf_op jit(solution)/shard_map/ppermute | solution.py:39
  101.0 3.0 %collective-permute-start.18 = (bf16[512,256]{1,0:T(8,128)(2,1)S(1)}, bf16[512,256]{1,0:T(8,128)(2,1)S(1)}, u32[]{:S(2)}, u32[]{:S(2)}) collective-permute-start(bf16[512,256]{1,0:T(8,128)(2,1)S(1)} %slice.19), channel_id=1, source_target_pairs={{0,48},{16,0},{32,16},{48,32},{1,49},{17,1},{33,17},{49,33},{2,50}... | collective-permute-start | bytes 786440 | tf_op jit(solution)/shard_map/ppermute | solution.py:41
  104.0 0.1 collective-permute-start.17
  104.1 0.9 constant_dynamic-update-slice_fusion.3
  105.0 0.9 constant_dynamic-update-slice_fusion.2
  105.9 0.4 collective-permute-done.16
  106.3 0.9 constant_dynamic-update-slice_fusion.1
  107.2 4.9 %collective-permute-done.17 = bf16[512,256]{1,0:T(8,128)(2,1)S(1)} collective-permute-done((bf16[512,256]{1,0:T(8,128)(2,1)S(1)}, bf16[512,256]{1,0:T(8,128)(2,1)S(1)}, u32[]{:S(2)}, u32[]{:S(2)}) %collective-permute-start.17) | collective-permute-done | bytes 262176 | tf_op jit(solution)/shard_map/ppermute | solution.py:40
  112.1 0.8 constant_dynamic-update-slice_fusion
  112.9 0.7 constant_dynamic-update-slice_fusion.15.j_ref
  113.6 7.8 %dispatch.1 = (bf16[128,2048]{1,0:T(8,128)(2,1)}, bf16[1024,2048]{1,0:T(8,128)(2,1)}) custom-call(s32[1]{0:T(128)} %bitcast.3.place_ref.here_ref, bf16[1024,2048]{1,0:T(8,128)(2,1)} %constant_dynamic-update-slice_fusion.15.j_ref, bf16[128,2048]{1,0:T(8,128)(2,1)} %bitcast.36, bf16[8,2048,256]{2,1,0:T(8,128)(2,1)} %bitcast.28, ...), custom_call_target="tpu_custom_call" | custom-call | tf_op jit(solution)/shard_map/dispatch/pallas_call | solution.py:245
  121.4 7.3 %all-to-all-start = ((bf16[128,8,2048]{2,1,0:T(8,128)(2,1)}), bf16[128,8,2048]{2,1,0:T(8,128)(2,1)}, u32[]{:S(2)}, u32[]{:S(2)}) async-start(bf16[128,8,2048]{2,1,0:T(8,128)(2,1)} %bitcast.30), calls=%async_computation | async-start | bytes 8388608 | tf_op jit(solution)/shard_map/all_to_all | solution.py:534
  128.7 0.3 reduce-scatter.2.cloned.1.call-start
  129.0 23.3 %shared.1 = bf16[1024,2048]{1,0:T(8,128)(2,1)} custom-call(bf16[1024,2048]{1,0:T(8,128)(2,1)} %constant_dynamic-update-slice_fusion.15.j_ref, bf16[1024,2048]{1,0:T(8,128)(2,1)} %constant_dynamic-update-slice_fusion.7.x_ref, bf16[8,2048,256]{2,1,0:T(8,128)(2,1)} %bitcast.29, bf16[1,2048]{1,0:T(2,128)(2,1)} %reshape.27.gain_ref, bf16[352,2048]{1,0:T(8,128)(2,1)} %bitcast.45, ...), custom_call_target="tpu_custom_call" | custom-call | flops 12999999488 | bytes 25000000 | tf_op jit(solution)/shard_map/shared/pallas_call | solution.py:326
  152.3 0.0 reduce-scatter.2.cloned.1.call-update
  152.3 38.7 %all-to-all-done = bf16[128,8,2048]{2,1,0:T(8,128)(2,1)} async-done(((bf16[128,8,2048]{2,1,0:T(8,128)(2,1)}), bf16[128,8,2048]{2,1,0:T(8,128)(2,1)}, u32[]{:S(2)}, u32[]{:S(2)}) %all-to-all-start) | async-done | bytes 4194336 | tf_op jit(solution)/shard_map/all_to_all | solution.py:534
  191.1 27.4 %experts.1 = bf16[1024,2048]{1,0:T(8,128)(2,1)} custom-call(bf16[1024,2048]{1,0:T(8,128)(2,1)} %bitcast.11.x_hbm, bf16[704,2048]{1,0:T(8,128)(2,1)} %bitcast.40, bf16[704,2048]{1,0:T(8,128)(2,1)} %bitcast.42, bf16[704,2048]{1,0:T(8,128)(2,1)} %bitcast.44, bf16[704,2048]{1,0:T(8,128)(2,1)} %collective-permute-done.8.g1, ...), custom_call_target="tpu_custom_call" | custom-call | flops 17699999744 | bytes 30000000 | tf_op jit(solution)/shard_map/experts/pallas_call | solution.py:408
  218.4 0.0 copy-start.1
  218.4 63.7 %all_to_all.10 = bf16[128,8,2048]{2,1,0:T(8,128)(2,1)} all-to-all(bf16[128,8,2048]{2,1,0:T(8,128)(2,1)} %bitcast.31), channel_id=1, replica_groups=mesh['xl'=2,'z'=4,'xh'=2,'y'=4,'c'=2] {'xl','z','xh','y','c'}, dimensions={0} | all-to-all | bytes 8388608 | tf_op jit(solution)/shard_map/all_to_all | solution.py:556
  282.1 5.3 %combine.1 = bf16[128,2048]{1,0:T(8,128)(2,1)} custom-call(bf16[384,1024]{1,0:T(8,128)(2,1)} %get-tuple-element.28.m_ref, bf16[1024,2048]{1,0:T(8,128)(2,1)} %bitcast.27, bf16[128,2048]{1,0:T(8,128)(2,1)} %get-tuple-element.46.resid_ref, bf16[128,2048]{1,0:T(8,128)(2,1)} %reduce-scatter.2.cloned.1.call-done.shared_ref), custom_call_target="tpu_custom_call" | custom-call | tf_op jit(solution)/shard_map/combine/pallas_call | solution.py:286
  (23 shorter events, 0.1 us)
Async XLA Ops:
  6.5 5.5 %copy-start = (bf16[256,2048]{1,0:T(8,128)(2,1)S(1)}, bf16[256,2048]{1,0:T(8,128)(2,1)}, u32[]{:S(2)}) copy-start(bf16[256,2048]{1,0:T(8,128)(2,1)} %param.29) | copy-start | bytes 3145732
  6.5 47.9 %all-gather.4.cloned.1.call-start = ((), (), s32[]{:S(2)}) async-start(), calls=%async_computation.3 | async-start | bytes 1179648 | tf_op jit(solution)/shard_map/all_gather | solution.py:508
  6.5 15.7 %collective-permute-start = (bf16[128,2048]{1,0:T(8,128)(2,1)}, bf16[128,2048]{1,0:T(8,128)(2,1)S(1)}, u32[]{:S(2)}, u32[]{:S(2)}) collective-permute-start(bf16[128,2048]{1,0:T(8,128)(2,1)} %bitcast.32), channel_id=1, source_target_pairs={{0,64},{64,0},{1,65},{65,1},{2,66},{66,2},{3,67},{67,3},{4,68},{68... | collective-permute-start | bytes 1572872 | tf_op jit(solution)/shard_map/ppermute | solution.py:34
  8.0 16.4 %collective-permute-start.1 = (bf16[128,2048]{1,0:T(8,128)(2,1)}, bf16[128,2048]{1,0:T(8,128)(2,1)S(1)}, u32[]{:S(2)}, u32[]{:S(2)}) collective-permute-start(bf16[128,2048]{1,0:T(8,128)(2,1)} %bitcast.33), channel_id=1, source_target_pairs={{0,16},{16,32},{32,48},{48,0},{1,17},{17,33},{33,49},{49,1},{2,18}... | collective-permute-start | bytes 1572872 | tf_op jit(solution)/shard_map/ppermute | solution.py:32
  9.9 16.8 %collective-permute-start.2 = (bf16[128,2048]{1,0:T(8,128)(2,1)}, bf16[128,2048]{1,0:T(8,128)(2,1)S(1)}, u32[]{:S(2)}, u32[]{:S(2)}) collective-permute-start(bf16[128,2048]{1,0:T(8,128)(2,1)} %bitcast.34), channel_id=1, source_target_pairs={{0,48},{16,0},{32,16},{48,32},{1,49},{17,1},{33,17},{49,33},{2,50}... | collective-permute-start | bytes 1572872 | tf_op jit(solution)/shard_map/ppermute | solution.py:33
  12.8 100.8 %all-gather.6.cloned.1.call-start = ((), (), s32[]{:S(2)}) async-start(), calls=%async_computation.5 | async-start | bytes 9437184 | tf_op jit(solution)/shard_map/all_gather | solution.py:516
  22.2 21.0 %collective-permute-start.4 = (bf16[128,2048]{1,0:T(8,128)(2,1)S(1)}, bf16[128,2048]{1,0:T(8,128)(2,1)S(1)}, u32[]{:S(2)}, u32[]{:S(2)}) collective-permute-start(bf16[128,2048]{1,0:T(8,128)(2,1)S(1)} %collective-permute-done), channel_id=1, source_target_pairs={{0,48},{16,0},{32,16},{48,32},{1,49},{17,1},{33,17},{49,33},{2,50}... | collective-permute-start | bytes 1572872 | tf_op jit(solution)/shard_map/ppermute | solution.py:39
  24.5 24.2 %collective-permute-start.5 = (bf16[128,2048]{1,0:T(8,128)(2,1)S(1)}, bf16[128,2048]{1,0:T(8,128)(2,1)S(1)}, u32[]{:S(2)}, u32[]{:S(2)}) collective-permute-start(bf16[128,2048]{1,0:T(8,128)(2,1)S(1)} %collective-permute-done.1), channel_id=1, source_target_pairs={{0,16},{16,32},{32,48},{48,0},{1,17},{17,33},{33,49},{49,1},{2,18}... | collective-permute-start | bytes 1572872 | tf_op jit(solution)/shard_map/ppermute | solution.py:37
  24.5 18.7 %collective-permute-start.3 = (bf16[128,2048]{1,0:T(8,128)(2,1)S(1)}, bf16[128,2048]{1,0:T(8,128)(2,1)S(1)}, u32[]{:S(2)}, u32[]{:S(2)}) collective-permute-start(bf16[128,2048]{1,0:T(8,128)(2,1)S(1)} %collective-permute-done.1), channel_id=1, source_target_pairs={{0,64},{64,0},{1,65},{65,1},{2,66},{66,2},{3,67},{67,3},{4,68},{68... | collective-permute-start | bytes 1572872 | tf_op jit(solution)/shard_map/ppermute | solution.py:38
  43.1 9.9 %collective-permute-start.6 = (bf16[64,2048]{1,0:T(8,128)(2,1)S(1)}, bf16[64,2048]{1,0:T(8,128)(2,1)S(1)}, u32[]{:S(2)}, u32[]{:S(2)}) collective-permute-start(bf16[64,2048]{1,0:T(8,128)(2,1)S(1)} %slice.16), channel_id=1, source_target_pairs={{0,16},{16,32},{32,48},{48,0},{1,17},{17,33},{33,49},{49,1},{2,18}... | collective-permute-start | bytes 786440 | tf_op jit(solution)/shard_map/ppermute | solution.py:40
  43.3 10.5 %collective-permute-start.7 = (bf16[64,2048]{1,0:T(8,128)(2,1)S(1)}, bf16[64,2048]{1,0:T(8,128)(2,1)S(1)}, u32[]{:S(2)}, u32[]{:S(2)}) collective-permute-start(bf16[64,2048]{1,0:T(8,128)(2,1)S(1)} %slice.17), channel_id=1, source_target_pairs={{0,48},{16,0},{32,16},{48,32},{1,49},{17,1},{33,17},{49,33},{2,50}... | collective-permute-start | bytes 786440 | tf_op jit(solution)/shard_map/ppermute | solution.py:41
  54.5 18.3 %collective-permute-start.8 = (bf16[704,2048]{1,0:T(8,128)(2,1)}, bf16[704,2048]{1,0:T(8,128)(2,1)}, u32[]{:S(2)}, u32[]{:S(2)}) collective-permute-start(bf16[704,2048]{1,0:T(8,128)(2,1)} %bitcast.39), channel_id=1, source_target_pairs={{0,1},{1,0},{2,3},{3,2},{4,5},{5,4},{6,7},{7,6},{8,9},{9,8},{10,11... | collective-permute-start | bytes 8650760 | tf_op jit(solution)/shard_map/ppermute | solution.py:100
  54.6 18.2 %collective-permute-start.9 = (bf16[704,2048]{1,0:T(8,128)(2,1)}, bf16[704,2048]{1,0:T(8,128)(2,1)}, u32[]{:S(2)}, u32[]{:S(2)}) collective-permute-start(bf16[704,2048]{1,0:T(8,128)(2,1)} %bitcast.41), channel_id=1, source_target_pairs={{0,1},{1,0},{2,3},{3,2},{4,5},{5,4},{6,7},{7,6},{8,9},{9,8},{10,11... | collective-permute-start | bytes 8650760 | tf_op jit(solution)/shard_map/ppermute | solution.py:100
  55.1 17.7 %collective-permute-start.10 = (bf16[704,2048]{1,0:T(8,128)(2,1)}, bf16[704,2048]{1,0:T(8,128)(2,1)}, u32[]{:S(2)}, u32[]{:S(2)}) collective-permute-start(bf16[704,2048]{1,0:T(8,128)(2,1)} %bitcast.43), channel_id=1, source_target_pairs={{0,1},{1,0},{2,3},{3,2},{4,5},{5,4},{6,7},{7,6},{8,9},{9,8},{10,11... | collective-permute-start | bytes 8650760 | tf_op jit(solution)/shard_map/ppermute | solution.py:100
  72.8 14.5 %collective-permute-start.13 = (bf16[1024,256]{1,0:T(8,128)(2,1)}, bf16[1024,256]{1,0:T(8,128)(2,1)S(1)}, u32[]{:S(2)}, u32[]{:S(2)}) collective-permute-start(bf16[1024,256]{1,0:T(8,128)(2,1)} %attend.1.own_ref), channel_id=1, source_target_pairs={{0,64},{64,0},{1,65},{65,1},{2,66},{66,2},{3,67},{67,3},{4,68},{68... | collective-permute-start | bytes 1572872 | tf_op jit(solution)/shard_map/ppermute | solution.py:34
  73.6 15.5 %collective-permute-start.11 = (bf16[1024,256]{1,0:T(8,128)(2,1)}, bf16[1024,256]{1,0:T(8,128)(2,1)S(1)}, u32[]{:S(2)}, u32[]{:S(2)}) collective-permute-start(bf16[1024,256]{1,0:T(8,128)(2,1)} %attend.1.own_ref), channel_id=1, source_target_pairs={{0,16},{16,32},{32,48},{48,0},{1,17},{17,33},{33,49},{49,1},{2,18}... | collective-permute-start | bytes 1572872 | tf_op jit(solution)/shard_map/ppermute | solution.py:32
  73.7 19.5 %collective-permute-start.12 = (bf16[1024,256]{1,0:T(8,128)(2,1)}, bf16[1024,256]{1,0:T(8,128)(2,1)S(1)}, u32[]{:S(2)}, u32[]{:S(2)}) collective-permute-start(bf16[1024,256]{1,0:T(8,128)(2,1)} %attend.1.own_ref), channel_id=1, source_target_pairs={{0,48},{16,0},{32,16},{48,32},{1,49},{17,1},{33,17},{49,33},{2,50}... | collective-permute-start | bytes 1572872 | tf_op jit(solution)/shard_map/ppermute | solution.py:33
  87.4 13.6 %collective-permute-start.15 = (bf16[1024,256]{1,0:T(8,128)(2,1)S(1)}, bf16[1024,256]{1,0:T(8,128)(2,1)S(1)}, u32[]{:S(2)}, u32[]{:S(2)}) collective-permute-start(bf16[1024,256]{1,0:T(8,128)(2,1)S(1)} %collective-permute-done.13), channel_id=1, source_target_pairs={{0,48},{16,0},{32,16},{48,32},{1,49},{17,1},{33,17},{49,33},{2,50}... | collective-permute-start | bytes 1572872 | tf_op jit(solution)/shard_map/ppermute | solution.py:39
  89.1 14.9 %collective-permute-start.14 = (bf16[1024,256]{1,0:T(8,128)(2,1)S(1)}, bf16[1024,256]{1,0:T(8,128)(2,1)S(1)}, u32[]{:S(2)}, u32[]{:S(2)}) collective-permute-start(bf16[1024,256]{1,0:T(8,128)(2,1)S(1)} %collective-permute-done.11), channel_id=1, source_target_pairs={{0,64},{64,0},{1,65},{65,1},{2,66},{66,2},{3,67},{67,3},{4,68},{68... | collective-permute-start | bytes 1572872 | tf_op jit(solution)/shard_map/ppermute | solution.py:38
  92.3 14.1 %collective-permute-start.16 = (bf16[1024,256]{1,0:T(8,128)(2,1)S(1)}, bf16[1024,256]{1,0:T(8,128)(2,1)S(1)}, u32[]{:S(2)}, u32[]{:S(2)}) collective-permute-start(bf16[1024,256]{1,0:T(8,128)(2,1)S(1)} %collective-permute-done.11), channel_id=1, source_target_pairs={{0,16},{16,32},{32,48},{48,0},{1,17},{17,33},{33,49},{49,1},{2,18}... | collective-permute-start | bytes 1572872 | tf_op jit(solution)/shard_map/ppermute | solution.py:37
  101.0 11.9 %collective-permute-start.18 = (bf16[512,256]{1,0:T(8,128)(2,1)S(1)}, bf16[512,256]{1,0:T(8,128)(2,1)S(1)}, u32[]{:S(2)}, u32[]{:S(2)}) collective-permute-start(bf16[512,256]{1,0:T(8,128)(2,1)S(1)} %slice.19), channel_id=1, source_target_pairs={{0,48},{16,0},{32,16},{48,32},{1,49},{17,1},{33,17},{49,33},{2,50}... | collective-permute-start | bytes 786440 | tf_op jit(solution)/shard_map/ppermute | solution.py:41
  104.0 8.1 %collective-permute-start.17 = (bf16[512,256]{1,0:T(8,128)(2,1)S(1)}, bf16[512,256]{1,0:T(8,128)(2,1)S(1)}, u32[]{:S(2)}, u32[]{:S(2)}) collective-permute-start(bf16[512,256]{1,0:T(8,128)(2,1)S(1)} %slice.18), channel_id=1, source_target_pairs={{0,16},{16,32},{32,48},{48,0},{1,17},{17,33},{33,49},{49,1},{2,18}... | collective-permute-start | bytes 786440 | tf_op jit(solution)/shard_map/ppermute | solution.py:40
  121.4 69.7 %all-to-all-start = ((bf16[128,8,2048]{2,1,0:T(8,128)(2,1)}), bf16[128,8,2048]{2,1,0:T(8,128)(2,1)}, u32[]{:S(2)}, u32[]{:S(2)}) async-start(bf16[128,8,2048]{2,1,0:T(8,128)(2,1)} %bitcast.30), calls=%async_computation | async-start | bytes 8388608 | tf_op jit(solution)/shard_map/all_to_all | solution.py:534
  128.7 153.4 %reduce-scatter.2.cloned.1.call-start = ((), (), s32[]{:S(2)}) async-start(), calls=%async_computation.4 | async-start | bytes 4718592 | tf_op jit(solution)/shard_map/reduce_scatter | solution.py:548
  218.4 69.0 %copy-start.1 = (bf16[256,2048]{1,0:T(8,128)(2,1)S(1)}, bf16[256,2048]{1,0:T(8,128)(2,1)}, u32[]{:S(2)}) copy-start(bf16[256,2048]{1,0:T(8,128)(2,1)} %param.29) | copy-start | bytes 3145732
Sparse Core Ops, SparseCore 0:
  12.9 39.7 all-gather.3
  54.6 48.8 all-gather.5
  152.4 69.0 reduce-scatter.1
